TPU v7x, 256 devices: a whole 4x4x8 slice. The times are simulated.
256 devices in a mesh: uly: 32 (over y, z), blk: 8 (over x, core).
Axes of the slice: x: 4, y: 4, z: 8, core: 2. Of those that a mesh axis runs over, the one named last changes fastest.
Arguments:
- qkv: bfloat16 [65536, 6144], P(('blk', 'uly')), may hold values from -16 to 16
- tile_list: int32 [256, 8], P('blk'), may hold values from 0 to 255, as said below
Outputs:
- attended: bfloat16 [65536, 2048], P(('blk', 'uly'))
Inputs may be any that keep to these rules, and one draw needn't show every extreme that they name: Let the frame of tile t be t // 32, its row t % 32 // 4 and its column t % 4. Each row of tile_list names 8 distinct tiles: its own tile and others whose frame, row and column each differ from its own by at most one.
All inputs are finite; a program needn't handle non-finite values.
Results may differ from a plain program's by a relative error of at most 0.0047.
Values may be sent and summed in bfloat16 or wider, within the bound.
No kernel may reach another device: no remote copies, remote signals or barrier semaphores. Data moves between devices by JAX's collectives and lax.ppermute only.
A program may use at most 128 MiB of HBM per device.

v0:
```python
import math

import jax
import jax.numpy as jnp
from jax import lax
from jax.sharding import PartitionSpec as P

HEAD_DIM = 64


def with_halo(cells, sides, width):
    for axis, dim in sides:
        count = lax.axis_size(axis)
        ends = count - 1
        head = lax.slice_in_dim(cells, 0, width, axis=dim)
        tail = lax.slice_in_dim(cells, cells.shape[dim] - width, cells.shape[dim], axis=dim)
        cells = jnp.concatenate(
            [
                lax.ppermute(tail, axis, [(i, (i + 1) % count) for i in range(ends)]),
                cells,
                lax.ppermute(head, axis, [((i + 1) % count, i) for i in range(ends)]),
            ],
            axis=dim,
        )
    return cells


def attend_group(queries, window, listed, score_scale):
    picked = window[listed]
    head_width = queries.shape[-1]
    key_part = picked[..., :head_width]
    val_part = picked[..., head_width:]
    scores = (
        jnp.einsum("gqhd,gjkhd->ghqjk", queries, key_part, preferred_element_type=jnp.float32)
        * score_scale
    )
    row_max = jnp.max(scores, axis=(3, 4), keepdims=True)
    exponent = jnp.exp(scores - row_max)
    row_sum = jnp.sum(exponent, axis=(3, 4))
    weights = exponent.astype(jnp.bfloat16)
    summed = jnp.einsum("ghqjk,gjkhd->gqhd", weights, val_part, preferred_element_type=jnp.float32)
    return (summed / jnp.transpose(row_sum, (0, 2, 1))[..., None]).astype(jnp.bfloat16)


def on_device(qkv, tile_list):
    score_scale = HEAD_DIM ** (-0.5)
    token_count = qkv.shape[0]
    all_heads = qkv.shape[1] // (3 * HEAD_DIM)
    head_here = all_heads // lax.axis_size("uly")
    row_count = token_count * lax.axis_size("uly")
    by_head = lax.all_to_all(qkv, "uly", split_axis=1, concat_axis=0, tiled=True)
    by_head = by_head.reshape(row_count, head_here, 3 * HEAD_DIM)
    queries = by_head[:, :, :HEAD_DIM]
    keyvals = by_head[:, :, HEAD_DIM:]
    window = with_halo(keyvals, (("blk", 0),), row_count)
    frame_tiles = tile_list.shape[0]
    tile_len = row_count // frame_tiles
    first_tile = (lax.axis_index("blk") - 1) * frame_tiles
    window = window.reshape(window.shape[0] // tile_len, tile_len, head_here, 2 * HEAD_DIM)
    local_list = tile_list - first_tile
    group_size = math.gcd(frame_tiles, max(1, 512 // tile_len))
    query_groups = queries.reshape(
        frame_tiles // group_size, group_size, tile_len, head_here, HEAD_DIM
    )
    list_groups = local_list.reshape(frame_tiles // group_size, group_size, local_list.shape[1])

    def run_group(inputs):
        return attend_group(inputs[0], window, inputs[1], score_scale)

    result = lax.map(run_group, (query_groups, list_groups))
    result = result.reshape(row_count, head_here * HEAD_DIM)
    return lax.all_to_all(result, "uly", split_axis=0, concat_axis=1, tiled=True)


def solution(mesh):
    in_specs = (P(("blk", "uly"), None), P("blk", None))
    out_specs = P(("blk", "uly"), None)
    return jax.shard_map(
        on_device, mesh=mesh, in_specs=in_specs, out_specs=out_specs, check_vma=False
    )
```

profile of v0, /device:TPU:37, one launch (start us, length us, event | category | flops | bytes accessed | tf_op | source)
XLA Modules:
  0.0 287.4 jit_solution(14690780181215844168)
XLA Ops:
  3.2 82.5 %all_to_all.35 = bf16[256,32,192]{0,2,1:T(8,128)(2,1)S(1)} all-to-all(bf16[256,32,192]{0,2,1:T(8,128)(2,1)S(1)} %bitcast.74), channel_id=1, replica_groups=mesh['uly'=32,'blk'=8] {'uly'}, dimensions={1} | all-to-all | bytes 6291456 | tf_op jit(solution)/shard_map/all_to_all | solution.py:51
  89.1 4.2 %reshape.78 = bf16[8192,1,192]{0,2,1:T(8,128)(2,1)S(1)} reshape(bf16[32,256,192]{1,0,2:T(8,128)(2,1)} %copy.19) | data formatting | bytes 6291456 | tf_op jit(solution)/shard_map/reshape | solution.py:52
  94.8 4.7 %collective-permute-start.1 = (bf16[8192,1,128]{0,2,1:T(8,128)(2,1)}, bf16[8192,1,128]{0,2,1:T(8,128)(2,1)}, u32[]{:S(2)}, u32[]{:S(2)}) collective-permute-start(bf16[8192,1,128]{0,2,1:T(8,128)(2,1)} %slice.18), channel_id=1, source_target_pairs={{1,0},{2,1},{3,2},{4,3},{5,4},{6,5},{7,6},{9,8},{10,9},{11,10},{12... | collective-permute-start | bytes 6291464 | tf_op jit(solution)/shard_map/ppermute | solution.py:21
  105.3 19.4 %collective-permute-done.1 = bf16[8192,1,128]{0,2,1:T(8,128)(2,1)} collective-permute-done((bf16[8192,1,128]{0,2,1:T(8,128)(2,1)}, bf16[8192,1,128]{0,2,1:T(8,128)(2,1)}, u32[]{:S(2)}, u32[]{:S(2)}) %collective-permute-start.1) | collective-permute-done | bytes 2097184 | tf_op jit(solution)/shard_map/ppermute | solution.py:21
  125.5 5.8 %pad_maximum_fusion = bf16[24576,1,128]{0,2,1:T(8,128)(2,1)} fusion(bf16[8192,1,128]{0,2,1:T(8,128)(2,1)} %collective-permute-done.1, bf16[8192,1,128]{0,2,1:T(8,128)(2,1)} %slice.18, bf16[8192,1,128]{0,2,1:T(8,128)(2,1)} %collective-permute-done), kind=kLoop, calls=%fused_computation.19 | loop fusion | flops 18874368 | bytes 12582912 | tf_op jit(solution)/shard_map/concatenate | solution.py:17
  131.3 8.7 %copy.20 = bf16[24576,1,128]{2,0,1:T(8,128)(2,1)} copy(bf16[24576,1,128]{0,2,1:T(8,128)(2,1)} %pad_maximum_fusion) | data formatting | bytes 12582912 | tf_op jit(solution)/shard_map/concatenate | solution.py:17
  140.0 115.5 %while.10 = (s32[]{:T(128)}, bf16[16,2,256,1,64]{2,4,1,3,0:T(8,128)(2,1)}, s32[16,2,8]{2,1,0:T(2,128)S(1)}, bf16[96,256,1,128]{3,1,0,2:T(8,128)(2,1)}, bf16[16,2,256,1,64]{2,1,0,4,3:T(2,128)(2,1)S(1)}, /*index=5*/s32[]{:T(128)}) while((s32[]{:T(128)}, bf16[16,2,256,1,64]{2,4,1,3,0:T(8,128)(2,1)}, s32[16,2,8]{2,1,0:T(2,128)S(1)}, ...), condition=%wide.region_3.4_spmd, body=%wide.region_0.3_spmd.sunk | while | flops 276889664 | bytes 18102744 | solution.py:70
  140.2 3.5 %gather_fusion = bf16[16,256,128]{2,1,0:T(8,128)(2,1)S(1)} fusion(bf16[96,256,128]{2,1,0:T(8,128)(2,1)} %bitcast.72, s32[1024]{0:T(1024)S(1)} %pad_clamp_fusion.2), kind=kCustom, calls=%fused_computation.clone.1 | custom fusion | bytes 2097216 | tf_op jit(solution)/shard_map/while/body/eval_jaxpr/gather | solution.py:29
  147.4 3.5 %gather_fusion = bf16[16,256,128]{2,1,0:T(8,128)(2,1)S(1)} fusion(bf16[96,256,128]{2,1,0:T(8,128)(2,1)} %bitcast.72, s32[1024]{0:T(1024)S(1)} %pad_clamp_fusion.2), kind=kCustom, calls=%fused_computation.clone.1 | custom fusion | bytes 2097216 | tf_op jit(solution)/shard_map/while/body/eval_jaxpr/gather | solution.py:29
  154.6 3.5 %gather_fusion = bf16[16,256,128]{2,1,0:T(8,128)(2,1)S(1)} fusion(bf16[96,256,128]{2,1,0:T(8,128)(2,1)} %bitcast.72, s32[1024]{0:T(1024)S(1)} %pad_clamp_fusion.2), kind=kCustom, calls=%fused_computation.clone.1 | custom fusion | bytes 2097216 | tf_op jit(solution)/shard_map/while/body/eval_jaxpr/gather | solution.py:29
  161.8 3.5 %gather_fusion = bf16[16,256,128]{2,1,0:T(8,128)(2,1)S(1)} fusion(bf16[96,256,128]{2,1,0:T(8,128)(2,1)} %bitcast.72, s32[1024]{0:T(1024)S(1)} %pad_clamp_fusion.2), kind=kCustom, calls=%fused_computation.clone.1 | custom fusion | bytes 2097216 | tf_op jit(solution)/shard_map/while/body/eval_jaxpr/gather | solution.py:29
  169.0 3.5 %gather_fusion = bf16[16,256,128]{2,1,0:T(8,128)(2,1)S(1)} fusion(bf16[96,256,128]{2,1,0:T(8,128)(2,1)} %bitcast.72, s32[1024]{0:T(1024)S(1)} %pad_clamp_fusion.2), kind=kCustom, calls=%fused_computation.clone.1 | custom fusion | bytes 2097216 | tf_op jit(solution)/shard_map/while/body/eval_jaxpr/gather | solution.py:29
  176.2 3.5 %gather_fusion = bf16[16,256,128]{2,1,0:T(8,128)(2,1)S(1)} fusion(bf16[96,256,128]{2,1,0:T(8,128)(2,1)} %bitcast.72, s32[1024]{0:T(1024)S(1)} %pad_clamp_fusion.2), kind=kCustom, calls=%fused_computation.clone.1 | custom fusion | bytes 2097216 | tf_op jit(solution)/shard_map/while/body/eval_jaxpr/gather | solution.py:29
  183.4 3.5 %gather_fusion = bf16[16,256,128]{2,1,0:T(8,128)(2,1)S(1)} fusion(bf16[96,256,128]{2,1,0:T(8,128)(2,1)} %bitcast.72, s32[1024]{0:T(1024)S(1)} %pad_clamp_fusion.2), kind=kCustom, calls=%fused_computation.clone.1 | custom fusion | bytes 2097216 | tf_op jit(solution)/shard_map/while/body/eval_jaxpr/gather | solution.py:29
  190.7 3.5 %gather_fusion = bf16[16,256,128]{2,1,0:T(8,128)(2,1)S(1)} fusion(bf16[96,256,128]{2,1,0:T(8,128)(2,1)} %bitcast.72, s32[1024]{0:T(1024)S(1)} %pad_clamp_fusion.2), kind=kCustom, calls=%fused_computation.clone.1 | custom fusion | bytes 2097216 | tf_op jit(solution)/shard_map/while/body/eval_jaxpr/gather | solution.py:29
  197.9 3.5 %gather_fusion = bf16[16,256,128]{2,1,0:T(8,128)(2,1)S(1)} fusion(bf16[96,256,128]{2,1,0:T(8,128)(2,1)} %bitcast.72, s32[1024]{0:T(1024)S(1)} %pad_clamp_fusion.2), kind=kCustom, calls=%fused_computation.clone.1 | custom fusion | bytes 2097216 | tf_op jit(solution)/shard_map/while/body/eval_jaxpr/gather | solution.py:29
  205.1 3.5 %gather_fusion = bf16[16,256,128]{2,1,0:T(8,128)(2,1)S(1)} fusion(bf16[96,256,128]{2,1,0:T(8,128)(2,1)} %bitcast.72, s32[1024]{0:T(1024)S(1)} %pad_clamp_fusion.2), kind=kCustom, calls=%fused_computation.clone.1 | custom fusion | bytes 2097216 | tf_op jit(solution)/shard_map/while/body/eval_jaxpr/gather | solution.py:29
  212.3 3.5 %gather_fusion = bf16[16,256,128]{2,1,0:T(8,128)(2,1)S(1)} fusion(bf16[96,256,128]{2,1,0:T(8,128)(2,1)} %bitcast.72, s32[1024]{0:T(1024)S(1)} %pad_clamp_fusion.2), kind=kCustom, calls=%fused_computation.clone.1 | custom fusion | bytes 2097216 | tf_op jit(solution)/shard_map/while/body/eval_jaxpr/gather | solution.py:29
  219.5 3.5 %gather_fusion = bf16[16,256,128]{2,1,0:T(8,128)(2,1)S(1)} fusion(bf16[96,256,128]{2,1,0:T(8,128)(2,1)} %bitcast.72, s32[1024]{0:T(1024)S(1)} %pad_clamp_fusion.2), kind=kCustom, calls=%fused_computation.clone.1 | custom fusion | bytes 2097216 | tf_op jit(solution)/shard_map/while/body/eval_jaxpr/gather | solution.py:29
  226.7 3.5 %gather_fusion = bf16[16,256,128]{2,1,0:T(8,128)(2,1)S(1)} fusion(bf16[96,256,128]{2,1,0:T(8,128)(2,1)} %bitcast.72, s32[1024]{0:T(1024)S(1)} %pad_clamp_fusion.2), kind=kCustom, calls=%fused_computation.clone.1 | custom fusion | bytes 2097216 | tf_op jit(solution)/shard_map/while/body/eval_jaxpr/gather | solution.py:29
  234.0 3.5 %gather_fusion = bf16[16,256,128]{2,1,0:T(8,128)(2,1)S(1)} fusion(bf16[96,256,128]{2,1,0:T(8,128)(2,1)} %bitcast.72, s32[1024]{0:T(1024)S(1)} %pad_clamp_fusion.2), kind=kCustom, calls=%fused_computation.clone.1 | custom fusion | bytes 2097216 | tf_op jit(solution)/shard_map/while/body/eval_jaxpr/gather | solution.py:29
  241.2 3.5 %gather_fusion = bf16[16,256,128]{2,1,0:T(8,128)(2,1)S(1)} fusion(bf16[96,256,128]{2,1,0:T(8,128)(2,1)} %bitcast.72, s32[1024]{0:T(1024)S(1)} %pad_clamp_fusion.2), kind=kCustom, calls=%fused_computation.clone.1 | custom fusion | bytes 2097216 | tf_op jit(solution)/shard_map/while/body/eval_jaxpr/gather | solution.py:29
  248.4 3.5 %gather_fusion = bf16[16,256,128]{2,1,0:T(8,128)(2,1)S(1)} fusion(bf16[96,256,128]{2,1,0:T(8,128)(2,1)} %bitcast.72, s32[1024]{0:T(1024)S(1)} %pad_clamp_fusion.2), kind=kCustom, calls=%fused_computation.clone.1 | custom fusion | bytes 2097216 | tf_op jit(solution)/shard_map/while/body/eval_jaxpr/gather | solution.py:29
  255.5 30.5 %all_to_all.36 = bf16[32,256,64]{1,2,0:T(8,128)(2,1)S(1)} all-to-all(bf16[32,256,64]{1,2,0:T(8,128)(2,1)} %bitcast.76), channel_id=1, replica_groups=mesh['uly'=32,'blk'=8] {'uly'}, dimensions={0} | all-to-all | bytes 2097152 | tf_op jit(solution)/shard_map/all_to_all | solution.py:72
  (141 shorter events, 74.6 us)
Async XLA Ops:
  89.1 13.2 %copy-start = (s32[32,8]{0,1:T(8,128)S(1)}, s32[32,8]{0,1:T(8,128)}, u32[]{:S(2)}) copy-start(s32[32,8]{0,1:T(8,128)} %param.5) | copy-start | bytes 3076
  94.8 29.9 %collective-permute-start.1 = (bf16[8192,1,128]{0,2,1:T(8,128)(2,1)}, bf16[8192,1,128]{0,2,1:T(8,128)(2,1)}, u32[]{:S(2)}, u32[]{:S(2)}) collective-permute-start(bf16[8192,1,128]{0,2,1:T(8,128)(2,1)} %slice.18), channel_id=1, source_target_pairs={{1,0},{2,1},{3,2},{4,3},{5,4},{6,5},{7,6},{9,8},{10,9},{11,10},{12... | collective-permute-start | bytes 6291464 | tf_op jit(solution)/shard_map/ppermute | solution.py:21
  99.5 26.0 %collective-permute-start = (bf16[8192,1,128]{0,2,1:T(8,128)(2,1)}, bf16[8192,1,128]{0,2,1:T(8,128)(2,1)}, u32[]{:S(2)}, u32[]{:S(2)}) collective-permute-start(bf16[8192,1,128]{0,2,1:T(8,128)(2,1)} %slice.18), channel_id=1, source_target_pairs={{0,1},{1,2},{2,3},{3,4},{4,5},{5,6},{6,7},{8,9},{9,10},{10,11},{11... | collective-permute-start | bytes 6291464 | tf_op jit(solution)/shard_map/ppermute | solution.py:19
where the time goes:
time: 293 us; the launch traced here: 287 us
  blocking collectives  113 us (39%)
  local copies, waits for them, and re-layouts  92.8 us (32%)
  matrix products  36.3 us (12%)
  waiting for transfers between devices  20.2 us (7%)
  other arithmetic  17.2 us (6%)
  starting transfers between devices  7.47 us (3%)
    all_to_all x1, blocking collectives, on_device(): lax.all_to_all(qkv, 'uly', split_axis=1, concat_axis=0, tiled=True)  82.5 us
    gather x32, local copies, waits for them, and re-layouts, attend_group(): picked = window[listed]  65 us
    all_to_all x1, blocking collectives, on_device(): lax.all_to_all(result, 'uly', split_axis=0, concat_axis=1, tiled=True)  30.5 us
    dot_general x16, matrix products, attend_group(): jnp.einsum('ghqjk,gjkhd->gqhd', weights, val_part, preferred_element_type...  23.9 us
    ppermute x1, waiting for transfers between devices, with_halo(): lax.ppermute(head, axis, [((i + 1) % count, i) for i in range(ends)])  19.4 us
    dot_general x16, matrix products, attend_group(): jnp.einsum('gqhd,gjkhd->ghqjk', queries, key_part, preferred_element_type...  12.3 us
    reduce_sum x16, other arithmetic, attend_group(): row_sum = jnp.sum(exponent, axis=(3, 4))  11.2 us
    concatenate x1, local copies, waits for them, and re-layouts, with_halo(): jnp.concatenate([lax.ppermute(tail, axis, [(i, (i + 1) % count) for i in...  8.66 us
  transfers between devices with their start and end apart: 2, of which 2 were waited for; matrix products, arithmetic and copies ran while one was open for 1% of the time, Pallas kernels for 0%

commit v1 on v0

v1 whole, which is shorter than its diff:
```python
import jax
import jax.numpy as jnp
from jax import lax
from jax.experimental import pallas as pl
from jax.experimental.pallas import tpu as pltpu
from jax.sharding import PartitionSpec as P

HEAD_DIM = 64
PAIR = 2 * HEAD_DIM
LOG2E = 1.4426950408889634
SPLIT_HEADS = 8


def split_kernel(qkv_ref, kv_ref, q_ref):
    half = qkv_ref.shape[0] // 2
    for pair in range(kv_ref.shape[0] // 2):
        base = pair * 6 * HEAD_DIM
        for odd in range(2):
            col = base + odd * 3 * HEAD_DIM
            head = 2 * pair + odd
            kv_ref[head] = qkv_ref[:, col + HEAD_DIM : col + 3 * HEAD_DIM]
            q_ref[head] = jnp.concatenate(
                [qkv_ref[:half, col : col + HEAD_DIM], qkv_ref[half:, col : col + HEAD_DIM]], axis=1
            )


def split_heads(qkv):
    tokens, width = qkv.shape
    heads = width // (3 * HEAD_DIM)
    group = SPLIT_HEADS
    return pl.pallas_call(
        split_kernel,
        grid=(heads // group,),
        in_specs=[pl.BlockSpec((tokens, group * 3 * HEAD_DIM), lambda i: (0, i))],
        out_specs=[
            pl.BlockSpec((group, tokens, PAIR), lambda i: (i, 0, 0)),
            pl.BlockSpec((group, tokens // 2, PAIR), lambda i: (i, 0, 0)),
        ],
        out_shape=[
            jax.ShapeDtypeStruct((heads, tokens, PAIR), qkv.dtype),
            jax.ShapeDtypeStruct((heads, tokens // 2, PAIR), qkv.dtype),
        ],
        name="split_heads",
    )(qkv)


def merge_kernel(o_ref, out_ref):
    half = o_ref.shape[1]
    for pair in range(o_ref.shape[0] // 2):
        even = o_ref[2 * pair]
        odd = o_ref[2 * pair + 1]
        cols = slice(pair * PAIR, (pair + 1) * PAIR)
        out_ref[:half, cols] = jnp.concatenate([even[:, :HEAD_DIM], odd[:, :HEAD_DIM]], axis=1)
        out_ref[half:, cols] = jnp.concatenate([even[:, HEAD_DIM:], odd[:, HEAD_DIM:]], axis=1)


def merge_heads(parts):
    heads, half, _ = parts.shape
    group = SPLIT_HEADS
    return pl.pallas_call(
        merge_kernel,
        grid=(heads // group,),
        in_specs=[pl.BlockSpec((group, half, PAIR), lambda i: (i, 0, 0))],
        out_specs=pl.BlockSpec((2 * half, group * HEAD_DIM), lambda i: (0, i)),
        out_shape=jax.ShapeDtypeStruct((2 * half, heads * HEAD_DIM), parts.dtype),
        name="merge_heads",
    )(parts)


def attend_kernel(list_ref, q_ref, prev_ref, own_ref, next_ref, o_ref, raw, keys, vals, sems):
    step = pl.program_id(0)
    frame_tiles = own_ref.shape[0]
    window = 3 * frame_tiles

    @pl.when(step == 0)
    def _():
        copies = [
            pltpu.make_async_copy(src, raw.at[pl.ds(i * frame_tiles, frame_tiles)], sems.at[i])
            for i, src in enumerate((prev_ref, own_ref, next_ref))
        ]
        for copy in copies:
            copy.start()
        for copy in copies:
            copy.wait()

        def prepare(t, carry):
            kv = raw[t]
            low = lax.broadcasted_iota(jnp.int32, kv.shape, 1) < HEAD_DIM
            keys[t] = jnp.where(low, kv, pltpu.roll(kv.astype(jnp.float32), HEAD_DIM, 1).astype(kv.dtype))
            vals[t] = jnp.where(low, jnp.ones_like(kv), kv)
            return carry

        lax.fori_loop(0, window, prepare, 0)

    packed = q_ref[0].astype(jnp.float32) * (HEAD_DIM**-0.5 * LOG2E)
    scaled = jnp.concatenate([packed[:, :HEAD_DIM], packed[:, HEAD_DIM:]], axis=0)
    coarse = scaled.astype(jnp.bfloat16)
    fine = (scaled - coarse.astype(jnp.float32)).astype(jnp.bfloat16)
    query = jnp.concatenate([coarse, fine], axis=1)
    listed = [list_ref[step, j] for j in range(list_ref.shape[1])]
    scores = [
        lax.dot_general(query, keys[t], (((1,), (1,)), ((), ())), preferred_element_type=jnp.float32)
        for t in listed
    ]
    top = scores[0]
    for s in scores[1:]:
        top = jnp.maximum(top, s)
    row_max = jnp.max(top, axis=1, keepdims=True)
    total = None
    for s, t in zip(scores, listed):
        weights = jnp.exp2(s - row_max).astype(jnp.bfloat16)
        part = jnp.dot(weights, vals[t], preferred_element_type=jnp.float32)
        total = part if total is None else total + part
    out = (total[:, HEAD_DIM:] / total[:, :HEAD_DIM]).astype(o_ref.dtype)
    half = out.shape[0] // 2
    o_ref[0] = jnp.concatenate([out[:half], out[half:]], axis=1)


def attend(local_list, queries, before, own, after):
    tiles, half, _ = queries.shape
    tile_len = own.shape[1]
    hbm = pl.BlockSpec(memory_space=pl.ANY)
    window = (3 * tiles, tile_len, PAIR)
    return pl.pallas_call(
        attend_kernel,
        grid_spec=pltpu.PrefetchScalarGridSpec(
            num_scalar_prefetch=1,
            grid=(tiles,),
            in_specs=[pl.BlockSpec((1, half, PAIR), lambda i, _: (i, 0, 0)), hbm, hbm, hbm],
            out_specs=pl.BlockSpec((1, half, PAIR), lambda i, _: (i, 0, 0)),
            scratch_shapes=[
                pltpu.VMEM(window, jnp.bfloat16),
                pltpu.VMEM(window, jnp.bfloat16),
                pltpu.VMEM(window, jnp.bfloat16),
                pltpu.SemaphoreType.DMA((3,)),
            ],
        ),
        out_shape=jax.ShapeDtypeStruct(queries.shape, queries.dtype),
        compiler_params=pltpu.CompilerParams(vmem_limit_bytes=48 * 2**20),
        name="attend",
    )(local_list, queries, before, own, after)


def on_device(qkv, tile_list):
    frames = lax.axis_size("blk")
    kv, queries = split_heads(qkv)
    kv = lax.all_to_all(kv, "uly", split_axis=0, concat_axis=0, tiled=True)
    up = [(i, i + 1) for i in range(frames - 1)]
    down = [(i + 1, i) for i in range(frames - 1)]
    before = lax.ppermute(kv, "blk", up)
    after = lax.ppermute(kv, "blk", down)
    queries, kv = lax.optimization_barrier((queries, kv))
    queries = lax.all_to_all(queries, "uly", split_axis=0, concat_axis=0, tiled=True)
    local_list = tile_list - (lax.axis_index("blk") - 1) * tile_list.shape[0]
    result = attend(local_list, queries, before, kv, after)
    result = lax.all_to_all(result, "uly", split_axis=0, concat_axis=0, tiled=True)
    return merge_heads(result)


def solution(mesh):
    in_specs = (P(("blk", "uly"), None), P("blk", None))
    out_specs = P(("blk", "uly"), None)
    return jax.shard_map(
        on_device, mesh=mesh, in_specs=in_specs, out_specs=out_specs, check_vma=False
    )
```

time: 293 us -> 191 us (0.65)
  local copies, waits for them, and re-layouts: 92.8 us -> 0.08 us
  Pallas kernels: 0 us -> 54 us
  matrix products: 36.3 us -> 0 us
  blocking collectives: 113 us -> 92.9 us
  other arithmetic: 17.2 us -> 0.01 us
  waiting for transfers between devices: 20.2 us -> 28.4 us
  starting transfers between devices: 7.47 us -> 12.2 us
    gather x32 -> x0, local copies, waits for them, and re-layouts: 65 us -> none  [attend_group(): picked = window[listed]]
    pallas_call x0 -> x3, Pallas kernels: none -> 54 us  [the longest x1 45.8 us: attend(): pl.pallas_call(attend_kernel, grid_spec=pltpu.PrefetchScalarGridSpec(num_...]
    dot_general x32 -> x0, matrix products: 36.3 us -> none  [the longest x16 23.9 us: attend_group(): jnp.einsum('ghqjk,gjkhd->gqhd', weights, val_part, preferred_element_type...]
    all_to_all x0 -> x1, waiting for transfers between devices: none -> 28.4 us  [on_device(): lax.all_to_all(queries, 'uly', split_axis=0, concat_axis=0, tiled=True)]
    ppermute x2, waiting for transfers between devices: 20.2 us -> 0.01 us  [the longest x1 0.01 us: on_device(): after = lax.ppermute(kv, 'blk', down)]
    all_to_all x2, blocking collectives: 113 us -> 92.9 us  [the longest x1 60.3 us: on_device(): kv = lax.all_to_all(kv, 'uly', split_axis=0, concat_axis=0, tiled=True)]
    reduce_sum x16 -> x0, other arithmetic: 11.2 us -> none  [attend_group(): row_sum = jnp.sum(exponent, axis=(3, 4))]
    concatenate x1 -> x0, local copies, waits for them, and re-layouts: 8.66 us -> none  [with_halo(): jnp.concatenate([lax.ppermute(tail, axis, [(i, (i + 1) % count) for i in...]
  transfers between devices with their start and end apart: 2 -> 3, of which waited for: 2 -> 1; matrix products, arithmetic and copies ran while one was open for 1% -> 0% of each run, Pallas kernels for 0% -> 0%
where the time goes in v1:
time: 191 us; the launch traced here: 188 us
  blocking collectives  92.9 us (49%)
  Pallas kernels  54 us (28%)
  waiting for transfers between devices  28.4 us (15%)
  starting transfers between devices  12.2 us (6%)
    all_to_all x1, blocking collectives, on_device(): kv = lax.all_to_all(kv, 'uly', split_axis=0, concat_axis=0, tiled=True)  60.3 us
    pallas_call x1, Pallas kernels, attend(): pl.pallas_call(attend_kernel, grid_spec=pltpu.PrefetchScalarGridSpec(num_...  45.8 us
    all_to_all x1, blocking collectives, on_device(): lax.all_to_all(result, 'uly', split_axis=0, concat_axis=0, tiled=True)  32.6 us
    all_to_all x1, waiting for transfers between devices, on_device(): lax.all_to_all(queries, 'uly', split_axis=0, concat_axis=0, tiled=True)  28.4 us
    ppermute x1, starting transfers between devices, on_device(): after = lax.ppermute(kv, 'blk', down)  4.88 us
    all_to_all x1, starting transfers between devices, on_device(): lax.all_to_all(queries, 'uly', split_axis=0, concat_axis=0, tiled=True)  4.64 us
    pallas_call x1, Pallas kernels, split_heads(): pl.pallas_call(split_kernel, grid=(heads // group,), in_specs=[pl.BlockSp...  4.59 us
  transfers between devices with their start and end apart: 3, of which 1 were waited for; matrix products, arithmetic and copies ran while one was open for 0% of the time, Pallas kernels for 0%

profile of v1, /device:TPU:37, one launch (start us, length us, event | category | flops | bytes accessed | tf_op | source)
XLA Modules:
  0.0 187.7 jit_solution(12087583036746113181)
XLA Ops:
  0.0 4.6 %split_heads.1 = (bf16[32,256,128]{2,1,0:T(8,128)(2,1)}, bf16[32,128,128]{2,1,0:T(8,128)(2,1)}) custom-call(bf16[256,6144]{1,0:T(8,128)(2,1)} %qkv_ref.1), custom_call_target="tpu_custom_call" | custom-call | tf_op jit(solution)/shard_map/split_heads/pallas_call | solution.py:31
  4.6 60.3 %all_to_all.15.own_ref = bf16[32,256,128]{2,1,0:T(8,128)(2,1)} all-to-all(bf16[32,256,128]{2,1,0:T(8,128)(2,1)} %get-tuple-element.10), channel_id=1, replica_groups=mesh['uly'=32,'blk'=8] {'uly'}, dimensions={0} | all-to-all | bytes 4194304 | tf_op jit(solution)/shard_map/all_to_all | solution.py:147
  64.9 0.0 copy-start
  64.9 4.9 %collective-permute-start.1 = (bf16[32,256,128]{2,1,0:T(8,128)(2,1)}, bf16[32,256,128]{2,1,0:T(8,128)(2,1)}, u32[]{:S(2)}, u32[]{:S(2)}) collective-permute-start(bf16[32,256,128]{2,1,0:T(8,128)(2,1)} %all_to_all.15.own_ref), channel_id=1, source_target_pairs={{1,0},{2,1},{3,2},{4,3},{5,4},{6,5},{7,6},{9,8},{10,9},{11,10},{12... | collective-permute-start | bytes 6291464 | tf_op jit(solution)/shard_map/ppermute | solution.py:151
  69.8 2.7 %collective-permute-start = (bf16[32,256,128]{2,1,0:T(8,128)(2,1)}, bf16[32,256,128]{2,1,0:T(8,128)(2,1)S(1)}, u32[]{:S(2)}, u32[]{:S(2)}) collective-permute-start(bf16[32,256,128]{2,1,0:T(8,128)(2,1)} %all_to_all.15.own_ref), channel_id=1, source_target_pairs={{0,1},{1,2},{2,3},{3,4},{4,5},{5,6},{6,7},{8,9},{9,10},{10,11},{11... | collective-permute-start | bytes 6291464 | tf_op jit(solution)/shard_map/ppermute | solution.py:150
  72.5 4.6 %all-to-all-start.1 = ((bf16[32,128,128]{2,1,0:T(8,128)(2,1)}), bf16[32,128,128]{2,1,0:T(8,128)(2,1)S(1)}, u32[]{:S(2)}, u32[]{:S(2)}) async-start(bf16[32,128,128]{2,1,0:T(8,128)(2,1)} %get-tuple-element.11), calls=%async_computation.1 | async-start | bytes 2097152 | tf_op jit(solution)/shard_map/all_to_all | solution.py:153
  77.1 0.0 copy-done
  77.2 0.1 copy.4
  77.2 28.4 %all-to-all-done.1.q_ref = bf16[32,128,128]{2,1,0:T(8,128)(2,1)S(1)} async-done(((bf16[32,128,128]{2,1,0:T(8,128)(2,1)}), bf16[32,128,128]{2,1,0:T(8,128)(2,1)S(1)}, u32[]{:S(2)}, u32[]{:S(2)}) %all-to-all-start.1) | async-done | bytes 1048608 | tf_op jit(solution)/shard_map/all_to_all | solution.py:153
  105.7 0.0 collective-permute-done.1.next_ref
  105.7 0.0 collective-permute-done.prev_ref
  105.7 45.8 %attend.1 = bf16[32,128,128]{2,1,0:T(8,128)(2,1)S(1)} custom-call(s32[32,8]{1,0:T(8,128)S(1)} %broadcast_subtract_fusion.list_ref, bf16[32,128,128]{2,1,0:T(8,128)(2,1)S(1)} %all-to-all-done.1.q_ref, bf16[32,256,128]{2,1,0:T(8,128)(2,1)S(1)} %collective-permute-done.prev_ref, bf16[32,256,128]{2,1,0:T(8,128)(2,1)} %all_to_all.15.own_ref, ...), custom_call_target="tpu_custom_call" | custom-call | tf_op jit(solution)/shard_map/attend/pallas_call | solution.py:124
  151.5 32.6 %all_to_all.16.o_ref = bf16[32,128,128]{2,1,0:T(8,128)(2,1)} all-to-all(bf16[32,128,128]{2,1,0:T(8,128)(2,1)S(1)} %attend.1), channel_id=1, replica_groups=mesh['uly'=32,'blk'=8] {'uly'}, dimensions={0} | all-to-all | bytes 2097152 | tf_op jit(solution)/shard_map/all_to_all | solution.py:156
  184.1 3.6 %merge_heads.1 = bf16[256,2048]{1,0:T(8,128)(2,1)} custom-call(bf16[32,128,128]{2,1,0:T(8,128)(2,1)} %all_to_all.16.o_ref), custom_call_target="tpu_custom_call" | custom-call | tf_op jit(solution)/shard_map/merge_heads/pallas_call | solution.py:60
  (1 shorter events, 0.0 us)
Async XLA Ops:
  64.9 12.3 %copy-start = (s32[32,8]{0,1:T(8,128)S(1)}, s32[32,8]{0,1:T(8,128)}, u32[]{:S(2)}) copy-start(s32[32,8]{0,1:T(8,128)} %param.3) | copy-start | bytes 3076
  64.9 40.8 %collective-permute-start.1 = (bf16[32,256,128]{2,1,0:T(8,128)(2,1)}, bf16[32,256,128]{2,1,0:T(8,128)(2,1)}, u32[]{:S(2)}, u32[]{:S(2)}) collective-permute-start(bf16[32,256,128]{2,1,0:T(8,128)(2,1)} %all_to_all.15.own_ref), channel_id=1, source_target_pairs={{1,0},{2,1},{3,2},{4,3},{5,4},{6,5},{7,6},{9,8},{10,9},{11,10},{12... | collective-permute-start | bytes 6291464 | tf_op jit(solution)/shard_map/ppermute | solution.py:151
  69.8 35.9 %collective-permute-start = (bf16[32,256,128]{2,1,0:T(8,128)(2,1)}, bf16[32,256,128]{2,1,0:T(8,128)(2,1)S(1)}, u32[]{:S(2)}, u32[]{:S(2)}) collective-permute-start(bf16[32,256,128]{2,1,0:T(8,128)(2,1)} %all_to_all.15.own_ref), channel_id=1, source_target_pairs={{0,1},{1,2},{2,3},{3,4},{4,5},{5,6},{6,7},{8,9},{9,10},{10,11},{11... | collective-permute-start | bytes 6291464 | tf_op jit(solution)/shard_map/ppermute | solution.py:150
  72.5 33.2 %all-to-all-start.1 = ((bf16[32,128,128]{2,1,0:T(8,128)(2,1)}), bf16[32,128,128]{2,1,0:T(8,128)(2,1)S(1)}, u32[]{:S(2)}, u32[]{:S(2)}) async-start(bf16[32,128,128]{2,1,0:T(8,128)(2,1)} %get-tuple-element.11), calls=%async_computation.1 | async-start | bytes 2097152 | tf_op jit(solution)/shard_map/all_to_all | solution.py:153

commit v2 on v1

--- a/solution.py
+++ b/solution.py
@@ -7,8 +7,8 @@
 
 HEAD_DIM = 64
 PAIR = 2 * HEAD_DIM
-LOG2E = 1.4426950408889634
-SPLIT_HEADS = 8
+SPLIT_HEADS = 16
+STEP_TILES = 8
 
 
 def split_kernel(qkv_ref, kv_ref, q_ref):
@@ -67,71 +67,79 @@
     )(parts)
 
 
-def attend_kernel(list_ref, q_ref, prev_ref, own_ref, next_ref, o_ref, raw, keys, vals, sems):
+def load_window(srcs, raw, sems):
+    tiles = srcs[0].shape[0]
+    copies = [
+        pltpu.make_async_copy(src, raw.at[pl.ds(i * tiles, tiles)], sems.at[i])
+        for i, src in enumerate(srcs)
+    ]
+    for copy in copies:
+        copy.start()
+    for copy in copies:
+        copy.wait()
+
+
+def padded_query(q_ref):
+    packed = q_ref * jnp.bfloat16(HEAD_DIM**-0.5)
+    stacked = jnp.concatenate([packed[:, :HEAD_DIM], packed[:, HEAD_DIM:]], axis=0)
+    return jnp.concatenate([stacked, jnp.zeros_like(stacked)], axis=1)
+
+
+def attend_kernel(list_ref, q_ref, prev_ref, own_ref, next_ref, o_ref, raw, sems):
     step = pl.program_id(0)
-    frame_tiles = own_ref.shape[0]
-    window = 3 * frame_tiles
 
     @pl.when(step == 0)
     def _():
-        copies = [
-            pltpu.make_async_copy(src, raw.at[pl.ds(i * frame_tiles, frame_tiles)], sems.at[i])
-            for i, src in enumerate((prev_ref, own_ref, next_ref))
+        load_window((prev_ref, own_ref, next_ref), raw, sems)
+
+    count = list_ref.shape[1]
+
+    def score(u):
+        query = padded_query(q_ref[u])
+        listed = [list_ref[step * q_ref.shape[0] + u, j] for j in range(count)]
+        dims = (((1,), (1,)), ((), ()))
+        scores = [
+            lax.dot_general(query, raw[t], dims, preferred_element_type=jnp.float32) for t in listed
         ]
-        for copy in copies:
-            copy.start()
-        for copy in copies:
-            copy.wait()
+        return listed, scores
 
-        def prepare(t, carry):
+    def finish(u, listed, scores):
+        top = scores[0]
+        for s in scores[1:]:
+            top = jnp.maximum(top, s)
+        row_max = jnp.max(top, axis=1, keepdims=True)
+        total = None
+        for s, t in zip(scores, listed):
+            weights = jnp.exp(s - row_max).astype(jnp.bfloat16)
             kv = raw[t]
             low = lax.broadcasted_iota(jnp.int32, kv.shape, 1) < HEAD_DIM
-            keys[t] = jnp.where(low, kv, pltpu.roll(kv.astype(jnp.float32), HEAD_DIM, 1).astype(kv.dtype))
-            vals[t] = jnp.where(low, jnp.ones_like(kv), kv)
-            return carry
+            ones_values = jnp.where(low, jnp.ones_like(kv), kv)
+            part = jnp.dot(weights, ones_values, preferred_element_type=jnp.float32)
+            total = part if total is None else total + part
+        out = (total[:, HEAD_DIM:] / total[:, :HEAD_DIM]).astype(o_ref.dtype)
+        half = out.shape[0] // 2
+        o_ref[u] = jnp.concatenate([out[:half], out[half:]], axis=1)
 
-        lax.fori_loop(0, window, prepare, 0)
-
-    packed = q_ref[0].astype(jnp.float32) * (HEAD_DIM**-0.5 * LOG2E)
-    scaled = jnp.concatenate([packed[:, :HEAD_DIM], packed[:, HEAD_DIM:]], axis=0)
-    coarse = scaled.astype(jnp.bfloat16)
-    fine = (scaled - coarse.astype(jnp.float32)).astype(jnp.bfloat16)
-    query = jnp.concatenate([coarse, fine], axis=1)
-    listed = [list_ref[step, j] for j in range(list_ref.shape[1])]
-    scores = [
-        lax.dot_general(query, keys[t], (((1,), (1,)), ((), ())), preferred_element_type=jnp.float32)
-        for t in listed
-    ]
-    top = scores[0]
-    for s in scores[1:]:
-        top = jnp.maximum(top, s)
-    row_max = jnp.max(top, axis=1, keepdims=True)
-    total = None
-    for s, t in zip(scores, listed):
-        weights = jnp.exp2(s - row_max).astype(jnp.bfloat16)
-        part = jnp.dot(weights, vals[t], preferred_element_type=jnp.float32)
-        total = part if total is None else total + part
-    out = (total[:, HEAD_DIM:] / total[:, :HEAD_DIM]).astype(o_ref.dtype)
-    half = out.shape[0] // 2
-    o_ref[0] = jnp.concatenate([out[:half], out[half:]], axis=1)
+    held = score(0)
+    for u in range(q_ref.shape[0]):
+        following = score(u + 1) if u + 1 < q_ref.shape[0] else None
+        finish(u, *held)
+        held = following
 
 
 def attend(local_list, queries, before, own, after):
     tiles, half, _ = queries.shape
     tile_len = own.shape[1]
     hbm = pl.BlockSpec(memory_space=pl.ANY)
-    window = (3 * tiles, tile_len, PAIR)
     return pl.pallas_call(
         attend_kernel,
         grid_spec=pltpu.PrefetchScalarGridSpec(
             num_scalar_prefetch=1,
-            grid=(tiles,),
-            in_specs=[pl.BlockSpec((1, half, PAIR), lambda i, _: (i, 0, 0)), hbm, hbm, hbm],
-            out_specs=pl.BlockSpec((1, half, PAIR), lambda i, _: (i, 0, 0)),
+            grid=(tiles // STEP_TILES,),
+            in_specs=[pl.BlockSpec((STEP_TILES, half, PAIR), lambda i, _: (i, 0, 0)), hbm, hbm, hbm],
+            out_specs=pl.BlockSpec((STEP_TILES, half, PAIR), lambda i, _: (i, 0, 0)),
             scratch_shapes=[
-                pltpu.VMEM(window, jnp.bfloat16),
-                pltpu.VMEM(window, jnp.bfloat16),
-                pltpu.VMEM(window, jnp.bfloat16),
+                pltpu.VMEM((3 * tiles, tile_len, PAIR), jnp.bfloat16),
                 pltpu.SemaphoreType.DMA((3,)),
             ],
         ),
@@ -149,7 +157,6 @@
     down = [(i + 1, i) for i in range(frames - 1)]
     before = lax.ppermute(kv, "blk", up)
     after = lax.ppermute(kv, "blk", down)
-    queries, kv = lax.optimization_barrier((queries, kv))
     queries = lax.all_to_all(queries, "uly", split_axis=0, concat_axis=0, tiled=True)
     local_list = tile_list - (lax.axis_index("blk") - 1) * tile_list.shape[0]
     result = attend(local_list, queries, before, kv, after)

time: 191 us -> 167 us (0.87)
  Pallas kernels: 54 us -> 30.9 us
    pallas_call x1, Pallas kernels: 45.8 us -> 25 us  [attend(): pl.pallas_call(attend_kernel, grid_spec=pltpu.PrefetchScalarGridSpec(num_...]
where the time goes in v2:
time: 167 us; the launch traced here: 165 us
  blocking collectives  92.9 us (56%)
  Pallas kernels  30.9 us (19%)
  waiting for transfers between devices  28.4 us (17%)
  starting transfers between devices  12.2 us (7%)
    all_to_all x1, blocking collectives, on_device(): kv = lax.all_to_all(kv, 'uly', split_axis=0, concat_axis=0, tiled=True)  60.3 us
    all_to_all x1, blocking collectives, on_device(): lax.all_to_all(result, 'uly', split_axis=0, concat_axis=0, tiled=True)  32.6 us
    all_to_all x1, waiting for transfers between devices, on_device(): lax.all_to_all(queries, 'uly', split_axis=0, concat_axis=0, tiled=True)  28.4 us
    pallas_call x1, Pallas kernels, attend(): pl.pallas_call(attend_kernel, grid_spec=pltpu.PrefetchScalarGridSpec(num_...  25 us
    ppermute x1, starting transfers between devices, on_device(): after = lax.ppermute(kv, 'blk', down)  4.88 us
    all_to_all x1, starting transfers between devices, on_device(): lax.all_to_all(queries, 'uly', split_axis=0, concat_axis=0, tiled=True)  4.64 us
    pallas_call x1, Pallas kernels, split_heads(): pl.pallas_call(split_kernel, grid=(heads // group,), in_specs=[pl.BlockSp...  3.59 us
  transfers between devices with their start and end apart: 3, of which 1 were waited for; matrix products, arithmetic and copies ran while one was open for 0% of the time, Pallas kernels for 0%

profile of v2, /device:TPU:37, one launch (start us, length us, event | category | flops | bytes accessed | tf_op | source)
XLA Modules:
  0.0 164.6 jit_solution(14463549665624227866)
XLA Ops:
  0.0 3.6 %split_heads.1 = (bf16[32,256,128]{2,1,0:T(8,128)(2,1)}, bf16[32,128,128]{2,1,0:T(8,128)(2,1)}) custom-call(bf16[256,6144]{1,0:T(8,128)(2,1)} %qkv_ref.1), custom_call_target="tpu_custom_call" | custom-call | tf_op jit(solution)/shard_map/split_heads/pallas_call | solution.py:31
  3.6 60.3 %all_to_all.15.own_ref = bf16[32,256,128]{2,1,0:T(8,128)(2,1)} all-to-all(bf16[32,256,128]{2,1,0:T(8,128)(2,1)} %get-tuple-element.8), channel_id=1, replica_groups=mesh['uly'=32,'blk'=8] {'uly'}, dimensions={0} | all-to-all | bytes 4194304 | tf_op jit(solution)/shard_map/all_to_all | solution.py:155
  63.9 0.0 copy-start
  63.9 4.9 %collective-permute-start.1 = (bf16[32,256,128]{2,1,0:T(8,128)(2,1)}, bf16[32,256,128]{2,1,0:T(8,128)(2,1)}, u32[]{:S(2)}, u32[]{:S(2)}) collective-permute-start(bf16[32,256,128]{2,1,0:T(8,128)(2,1)} %all_to_all.15.own_ref), channel_id=1, source_target_pairs={{1,0},{2,1},{3,2},{4,3},{5,4},{6,5},{7,6},{9,8},{10,9},{11,10},{12... | collective-permute-start | bytes 6291464 | tf_op jit(solution)/shard_map/ppermute | solution.py:159
  68.8 2.7 %collective-permute-start = (bf16[32,256,128]{2,1,0:T(8,128)(2,1)}, bf16[32,256,128]{2,1,0:T(8,128)(2,1)S(1)}, u32[]{:S(2)}, u32[]{:S(2)}) collective-permute-start(bf16[32,256,128]{2,1,0:T(8,128)(2,1)} %all_to_all.15.own_ref), channel_id=1, source_target_pairs={{0,1},{1,2},{2,3},{3,4},{4,5},{5,6},{6,7},{8,9},{9,10},{10,11},{11... | collective-permute-start | bytes 6291464 | tf_op jit(solution)/shard_map/ppermute | solution.py:158
  71.5 4.6 %all-to-all-start = ((bf16[32,128,128]{2,1,0:T(8,128)(2,1)}), bf16[32,128,128]{2,1,0:T(8,128)(2,1)S(1)}, u32[]{:S(2)}, u32[]{:S(2)}) async-start(bf16[32,128,128]{2,1,0:T(8,128)(2,1)} %get-tuple-element.7), calls=%async_computation | async-start | bytes 2097152 | tf_op jit(solution)/shard_map/all_to_all | solution.py:160
  76.1 0.0 copy-done
  76.2 0.1 copy.4
  76.2 28.4 %all-to-all-done.q_ref = bf16[32,128,128]{2,1,0:T(8,128)(2,1)S(1)} async-done(((bf16[32,128,128]{2,1,0:T(8,128)(2,1)}), bf16[32,128,128]{2,1,0:T(8,128)(2,1)S(1)}, u32[]{:S(2)}, u32[]{:S(2)}) %all-to-all-start) | async-done | bytes 1048608 | tf_op jit(solution)/shard_map/all_to_all | solution.py:160
  104.7 0.0 collective-permute-done.1.next_ref
  104.7 0.0 collective-permute-done.prev_ref
  104.7 25.0 %attend.1 = bf16[32,128,128]{2,1,0:T(8,128)(2,1)S(1)} custom-call(s32[32,8]{1,0:T(8,128)S(1)} %broadcast_subtract_fusion.list_ref, bf16[32,128,128]{2,1,0:T(8,128)(2,1)S(1)} %all-to-all-done.q_ref, bf16[32,256,128]{2,1,0:T(8,128)(2,1)S(1)} %collective-permute-done.prev_ref, bf16[32,256,128]{2,1,0:T(8,128)(2,1)} %all_to_all.15.own_ref, ...), custom_call_target="tpu_custom_call" | custom-call | tf_op jit(solution)/shard_map/attend/pallas_call | solution.py:134
  129.7 32.6 %all_to_all.16.o_ref = bf16[32,128,128]{2,1,0:T(8,128)(2,1)} all-to-all(bf16[32,128,128]{2,1,0:T(8,128)(2,1)S(1)} %attend.1), channel_id=1, replica_groups=mesh['uly'=32,'blk'=8] {'uly'}, dimensions={0} | all-to-all | bytes 2097152 | tf_op jit(solution)/shard_map/all_to_all | solution.py:163
  162.3 2.3 %merge_heads.1 = bf16[256,2048]{1,0:T(8,128)(2,1)} custom-call(bf16[32,128,128]{2,1,0:T(8,128)(2,1)} %all_to_all.16.o_ref), custom_call_target="tpu_custom_call" | custom-call | tf_op jit(solution)/shard_map/merge_heads/pallas_call | solution.py:60
  (1 shorter events, 0.0 us)
Async XLA Ops:
  63.9 12.3 %copy-start = (s32[32,8]{0,1:T(8,128)S(1)}, s32[32,8]{0,1:T(8,128)}, u32[]{:S(2)}) copy-start(s32[32,8]{0,1:T(8,128)} %param.3) | copy-start | bytes 3076
  63.9 40.8 %collective-permute-start.1 = (bf16[32,256,128]{2,1,0:T(8,128)(2,1)}, bf16[32,256,128]{2,1,0:T(8,128)(2,1)}, u32[]{:S(2)}, u32[]{:S(2)}) collective-permute-start(bf16[32,256,128]{2,1,0:T(8,128)(2,1)} %all_to_all.15.own_ref), channel_id=1, source_target_pairs={{1,0},{2,1},{3,2},{4,3},{5,4},{6,5},{7,6},{9,8},{10,9},{11,10},{12... | collective-permute-start | bytes 6291464 | tf_op jit(solution)/shard_map/ppermute | solution.py:159
  68.8 35.9 %collective-permute-start = (bf16[32,256,128]{2,1,0:T(8,128)(2,1)}, bf16[32,256,128]{2,1,0:T(8,128)(2,1)S(1)}, u32[]{:S(2)}, u32[]{:S(2)}) collective-permute-start(bf16[32,256,128]{2,1,0:T(8,128)(2,1)} %all_to_all.15.own_ref), channel_id=1, source_target_pairs={{0,1},{1,2},{2,3},{3,4},{4,5},{5,6},{6,7},{8,9},{9,10},{10,11},{11... | collective-permute-start | bytes 6291464 | tf_op jit(solution)/shard_map/ppermute | solution.py:158
  71.5 33.2 %all-to-all-start = ((bf16[32,128,128]{2,1,0:T(8,128)(2,1)}), bf16[32,128,128]{2,1,0:T(8,128)(2,1)S(1)}, u32[]{:S(2)}, u32[]{:S(2)}) async-start(bf16[32,128,128]{2,1,0:T(8,128)(2,1)} %get-tuple-element.7), calls=%async_computation | async-start | bytes 2097152 | tf_op jit(solution)/shard_map/all_to_all | solution.py:160

commit v3 on v2

--- a/solution.py
+++ b/solution.py
@@ -63,6 +63,7 @@
         in_specs=[pl.BlockSpec((group, half, PAIR), lambda i: (i, 0, 0))],
         out_specs=pl.BlockSpec((2 * half, group * HEAD_DIM), lambda i: (0, i)),
         out_shape=jax.ShapeDtypeStruct((2 * half, heads * HEAD_DIM), parts.dtype),
+        compiler_params=pltpu.CompilerParams(vmem_limit_bytes=8 * 2**20),
         name="merge_heads",
     )(parts)
 
@@ -144,7 +145,7 @@
             ],
         ),
         out_shape=jax.ShapeDtypeStruct(queries.shape, queries.dtype),
-        compiler_params=pltpu.CompilerParams(vmem_limit_bytes=48 * 2**20),
+        compiler_params=pltpu.CompilerParams(vmem_limit_bytes=32 * 2**20),
         name="attend",
     )(local_list, queries, before, own, after)
 
@@ -158,6 +159,7 @@
     before = lax.ppermute(kv, "blk", up)
     after = lax.ppermute(kv, "blk", down)
     queries = lax.all_to_all(queries, "uly", split_axis=0, concat_axis=0, tiled=True)
+    queries, tile_list = lax.optimization_barrier((queries, tile_list))
     local_list = tile_list - (lax.axis_index("blk") - 1) * tile_list.shape[0]
     result = attend(local_list, queries, before, kv, after)
     result = lax.all_to_all(result, "uly", split_axis=0, concat_axis=0, tiled=True)

time: 167 us -> 165 us (0.988)
  the two profiles are of different devices: /device:TPU:37 before, /device:TPU:2 now
where the time goes in v3:
time: 165 us
  blocking collectives  100 us (61%)
  Pallas kernels  29.8 us (18%)
  waiting for transfers between devices  25 us (15%)
  starting transfers between devices  9.54 us (6%)
    all_to_all x1, blocking collectives, on_device(): kv = lax.all_to_all(kv, 'uly', split_axis=0, concat_axis=0, tiled=True)  62.6 us
    all_to_all x1, blocking collectives, on_device(): lax.all_to_all(result, 'uly', split_axis=0, concat_axis=0, tiled=True)  37.7 us
    pallas_call x1, Pallas kernels, attend(): pl.pallas_call(attend_kernel, grid_spec=pltpu.PrefetchScalarGridSpec(num_...  24.9 us
    all_to_all x1, waiting for transfers between devices, on_device(): lax.all_to_all(queries, 'uly', split_axis=0, concat_axis=0, tiled=True)  24 us
    all_to_all x1, starting transfers between devices, on_device(): lax.all_to_all(queries, 'uly', split_axis=0, concat_axis=0, tiled=True)  5.21 us
    pallas_call x1, Pallas kernels, split_heads(): pl.pallas_call(split_kernel, grid=(heads // group,), in_specs=[pl.BlockSp...  3.59 us
  transfers between devices with their start and end apart: 3, of which 2 were waited for; matrix products, arithmetic and copies ran while one was open for 0% of the time, Pallas kernels for 0%

profile of v3, /device:TPU:2, one launch (start us, length us, event | category | flops | bytes accessed | tf_op | source)
XLA Modules:
  0.0 164.6 jit_solution(3978394594903158092)
XLA Ops:
  0.0 3.6 %split_heads.1 = (bf16[32,256,128]{2,1,0:T(8,128)(2,1)}, bf16[32,128,128]{2,1,0:T(8,128)(2,1)}) custom-call(bf16[256,6144]{1,0:T(8,128)(2,1)} %qkv_ref.1), custom_call_target="tpu_custom_call" | custom-call | tf_op jit(solution)/shard_map/split_heads/pallas_call | solution.py:31
  3.6 62.6 %all_to_all.15.own_ref = bf16[32,256,128]{2,1,0:T(8,128)(2,1)S(1)} all-to-all(bf16[32,256,128]{2,1,0:T(8,128)(2,1)} %get-tuple-element.12), channel_id=1, replica_groups=mesh['uly'=32,'blk'=8] {'uly'}, dimensions={0} | all-to-all | bytes 4194304 | tf_op jit(solution)/shard_map/all_to_all | solution.py:156
  66.2 0.0 copy-start
  66.2 5.2 %all-to-all-start = ((bf16[32,128,128]{2,1,0:T(8,128)(2,1)}), bf16[32,128,128]{2,1,0:T(8,128)(2,1)S(1)}, u32[]{:S(2)}, u32[]{:S(2)}) async-start(bf16[32,128,128]{2,1,0:T(8,128)(2,1)} %get-tuple-element.9), calls=%async_computation | async-start | bytes 2097152 | tf_op jit(solution)/shard_map/all_to_all | solution.py:161
  71.4 1.9 %collective-permute-start.1 = (bf16[32,256,128]{2,1,0:T(8,128)(2,1)S(1)}, bf16[32,256,128]{2,1,0:T(8,128)(2,1)}, u32[]{:S(2)}, u32[]{:S(2)}) collective-permute-start(bf16[32,256,128]{2,1,0:T(8,128)(2,1)S(1)} %all_to_all.15.own_ref), channel_id=1, source_target_pairs={{1,0},{2,1},{3,2},{4,3},{5,4},{6,5},{7,6},{9,8},{10,9},{11,10},{12... | collective-permute-start | bytes 6291464 | tf_op jit(solution)/shard_map/ppermute | solution.py:160
  73.3 2.4 %collective-permute-start = (bf16[32,256,128]{2,1,0:T(8,128)(2,1)S(1)}, bf16[32,256,128]{2,1,0:T(8,128)(2,1)}, u32[]{:S(2)}, u32[]{:S(2)}) collective-permute-start(bf16[32,256,128]{2,1,0:T(8,128)(2,1)S(1)} %all_to_all.15.own_ref), channel_id=1, source_target_pairs={{0,1},{1,2},{2,3},{3,4},{4,5},{5,6},{6,7},{8,9},{9,10},{10,11},{11... | collective-permute-start | bytes 6291464 | tf_op jit(solution)/shard_map/ppermute | solution.py:159
  75.8 24.0 %all-to-all-done.q_ref = bf16[32,128,128]{2,1,0:T(8,128)(2,1)S(1)} async-done(((bf16[32,128,128]{2,1,0:T(8,128)(2,1)}), bf16[32,128,128]{2,1,0:T(8,128)(2,1)S(1)}, u32[]{:S(2)}, u32[]{:S(2)}) %all-to-all-start) | async-done | bytes 1048608 | tf_op jit(solution)/shard_map/all_to_all | solution.py:161
  99.7 0.0 copy-done
  99.7 0.1 copy.4
  99.8 0.0 collective-permute-done.1.next_ref
  99.8 1.0 collective-permute-done.prev_ref
  100.8 24.9 %attend.1 = bf16[32,128,128]{2,1,0:T(8,128)(2,1)S(1)} custom-call(s32[32,8]{1,0:T(8,128)S(1)} %broadcast_subtract_fusion.list_ref, bf16[32,128,128]{2,1,0:T(8,128)(2,1)S(1)} %all-to-all-done.q_ref, bf16[32,256,128]{2,1,0:T(8,128)(2,1)} %collective-permute-done.prev_ref, bf16[32,256,128]{2,1,0:T(8,128)(2,1)S(1)} %all_to_all.15.own_ref, ...), custom_call_target="tpu_custom_call" | custom-call | tf_op jit(solution)/shard_map/attend/pallas_call | solution.py:135
  125.7 37.7 %all_to_all.16.o_ref = bf16[32,128,128]{2,1,0:T(8,128)(2,1)S(1)} all-to-all(bf16[32,128,128]{2,1,0:T(8,128)(2,1)S(1)} %attend.1), channel_id=1, replica_groups=mesh['uly'=32,'blk'=8] {'uly'}, dimensions={0} | all-to-all | bytes 2097152 | tf_op jit(solution)/shard_map/all_to_all | solution.py:165
  163.4 1.3 merge_heads.1
  (1 shorter events, 0.0 us)
Async XLA Ops:
  66.2 33.5 %copy-start = (s32[32,8]{0,1:T(8,128)S(1)}, s32[32,8]{0,1:T(8,128)}, u32[]{:S(2)}) copy-start(s32[32,8]{0,1:T(8,128)} %param.3) | copy-start | bytes 3076
  66.2 33.5 %all-to-all-start = ((bf16[32,128,128]{2,1,0:T(8,128)(2,1)}), bf16[32,128,128]{2,1,0:T(8,128)(2,1)S(1)}, u32[]{:S(2)}, u32[]{:S(2)}) async-start(bf16[32,128,128]{2,1,0:T(8,128)(2,1)} %get-tuple-element.9), calls=%async_computation | async-start | bytes 2097152 | tf_op jit(solution)/shard_map/all_to_all | solution.py:161
  71.4 28.4 %collective-permute-start.1 = (bf16[32,256,128]{2,1,0:T(8,128)(2,1)S(1)}, bf16[32,256,128]{2,1,0:T(8,128)(2,1)}, u32[]{:S(2)}, u32[]{:S(2)}) collective-permute-start(bf16[32,256,128]{2,1,0:T(8,128)(2,1)S(1)} %all_to_all.15.own_ref), channel_id=1, source_target_pairs={{1,0},{2,1},{3,2},{4,3},{5,4},{6,5},{7,6},{9,8},{10,9},{11,10},{12... | collective-permute-start | bytes 6291464 | tf_op jit(solution)/shard_map/ppermute | solution.py:160
  73.3 27.5 %collective-permute-start = (bf16[32,256,128]{2,1,0:T(8,128)(2,1)S(1)}, bf16[32,256,128]{2,1,0:T(8,128)(2,1)}, u32[]{:S(2)}, u32[]{:S(2)}) collective-permute-start(bf16[32,256,128]{2,1,0:T(8,128)(2,1)S(1)} %all_to_all.15.own_ref), channel_id=1, source_target_pairs={{0,1},{1,2},{2,3},{3,4},{4,5},{5,6},{6,7},{8,9},{9,10},{10,11},{11... | collective-permute-start | bytes 6291464 | tf_op jit(solution)/shard_map/ppermute | solution.py:159

commit v4 on v3

--- a/solution.py
+++ b/solution.py
@@ -150,20 +150,27 @@
     )(local_list, queries, before, own, after)
 
 
+def exchange(array):
+    return lax.all_to_all(array, "uly", split_axis=0, concat_axis=0, tiled=True)
+
+
 def on_device(qkv, tile_list):
     frames = lax.axis_size("blk")
+    frame = lax.axis_index("blk")
+    odd = frame % 2
     kv, queries = split_heads(qkv)
-    kv = lax.all_to_all(kv, "uly", split_axis=0, concat_axis=0, tiled=True)
-    up = [(i, i + 1) for i in range(frames - 1)]
-    down = [(i + 1, i) for i in range(frames - 1)]
-    before = lax.ppermute(kv, "blk", up)
-    after = lax.ppermute(kv, "blk", down)
-    queries = lax.all_to_all(queries, "uly", split_axis=0, concat_axis=0, tiled=True)
-    queries, tile_list = lax.optimization_barrier((queries, tile_list))
-    local_list = tile_list - (lax.axis_index("blk") - 1) * tile_list.shape[0]
-    result = attend(local_list, queries, before, kv, after)
-    result = lax.all_to_all(result, "uly", split_axis=0, concat_axis=0, tiled=True)
-    return merge_heads(result)
+    kv = exchange(kv)
+    far = lax.ppermute(kv, "blk", [p for i in range(1, frames - 1, 2) for p in ((i, i + 1), (i + 1, i))])
+    near = lax.ppermute(kv, "blk", [p for i in range(0, frames, 2) for p in ((i, i + 1), (i + 1, i))])
+    queries = lax.cond(odd == 0, exchange, lambda a: a, queries)
+    queries, near = lax.optimization_barrier((queries, near))
+    queries = lax.cond(odd == 1, exchange, lambda a: a, queries)
+    frame_tiles = tile_list.shape[0]
+    step = tile_list // frame_tiles - frame
+    slot = 1 + jnp.where(odd == 0, step, -step)
+    local_list = slot * frame_tiles + tile_list % frame_tiles
+    result = attend(local_list, queries, far, kv, near)
+    return merge_heads(exchange(result))
 
 
 def solution(mesh):

time: 165 us -> 164 us (level)
  the two profiles are of different devices: /device:TPU:2 before, /device:TPU:37 now
where the time goes in v4:
time: 164 us; the launch traced here: 162 us
  blocking collectives  125 us (76%)
  Pallas kernels  29.6 us (18%)
  starting transfers between devices  5.55 us (3%)
    all_to_all x3, blocking collectives, exchange(): return lax.all_to_all(array, 'uly', split_axis=0, concat_axis=0, tiled=True)  125 us
    pallas_call x1, Pallas kernels, attend(): pl.pallas_call(attend_kernel, grid_spec=pltpu.PrefetchScalarGridSpec(num_...  24.9 us
    pallas_call x1, Pallas kernels, split_heads(): pl.pallas_call(split_kernel, grid=(heads // group,), in_specs=[pl.BlockSp...  3.47 us
  transfers between devices with their start and end apart: 2, of which 1 were waited for; matrix products, arithmetic and copies ran while one was open for 0% of the time, Pallas kernels for 0%

profile of v4, /device:TPU:37, one launch (start us, length us, event | category | flops | bytes accessed | tf_op | source)
XLA Modules:
  0.0 161.7 jit_solution(10815294485249740388)
XLA Ops:
  0.0 3.5 %split_heads.1 = (bf16[32,256,128]{2,1,0:T(8,128)(2,1)}, bf16[32,128,128]{2,1,0:T(8,128)(2,1)S(1)}) custom-call(bf16[256,6144]{1,0:T(8,128)(2,1)} %qkv_ref.1), custom_call_target="tpu_custom_call" | custom-call | tf_op jit(solution)/shard_map/split_heads/pallas_call | solution.py:31
  3.5 0.0 copy-start
  3.5 60.3 %all_to_all.20.own_ref = bf16[32,256,128]{2,1,0:T(8,128)(2,1)S(1)} all-to-all(bf16[32,256,128]{2,1,0:T(8,128)(2,1)} %get-tuple-element.20), channel_id=1, replica_groups=mesh['uly'=32,'blk'=8] {'uly'}, dimensions={0} | all-to-all | bytes 4194304 | tf_op jit(solution)/shard_map/all_to_all | solution.py:154
  63.8 2.8 %collective-permute-start = (bf16[32,256,128]{2,1,0:T(8,128)(2,1)S(1)}, bf16[32,256,128]{2,1,0:T(8,128)(2,1)}, u32[]{:S(2)}, u32[]{:S(2)}) collective-permute-start(bf16[32,256,128]{2,1,0:T(8,128)(2,1)S(1)} %all_to_all.20.own_ref), channel_id=1, source_target_pairs={{0,1},{1,0},{2,3},{3,2},{4,5},{5,4},{6,7},{7,6},{8,9},{9,8},{10,11... | collective-permute-start | bytes 6291464 | tf_op jit(solution)/shard_map/ppermute | solution.py:164
  66.6 2.7 %collective-permute-start.1 = (bf16[32,256,128]{2,1,0:T(8,128)(2,1)S(1)}, bf16[32,256,128]{2,1,0:T(8,128)(2,1)}, u32[]{:S(2)}, u32[]{:S(2)}) collective-permute-start(bf16[32,256,128]{2,1,0:T(8,128)(2,1)S(1)} %all_to_all.20.own_ref), channel_id=1, source_target_pairs={{1,2},{2,1},{3,4},{4,3},{5,6},{6,5},{9,10},{10,9},{11,12},{12,11},... | collective-permute-start | bytes 6291464 | tf_op jit(solution)/shard_map/ppermute | solution.py:163
  69.4 0.0 copy-done
  69.4 0.1 copy.3
  69.5 1.1 collective-permute-done.next_ref
  70.6 32.7 %conditional.3 = (bf16[32,128,128]{2,1,0:T(8,128)(2,1)S(1)}) conditional(s32[]{:T(128)} %convert_element_type.6, bf16[32,128,128]{2,1,0:T(8,128)(2,1)S(1)} %get-tuple-element.23, bf16[32,128,128]{2,1,0:T(8,128)(2,1)S(1)} %get-tuple-element.23), branch_computations={%region_2.3_spmd, %region_3.4_spmd} | conditional | bytes 4194312 | solution.py:167
  70.6 0.1 copy.12
  70.6 32.6 %all_to_all.19 = bf16[32,128,128]{2,1,0:T(8,128)(2,1)S(1)} all-to-all(bf16[32,128,128]{2,1,0:T(8,128)(2,1)S(1)} %copy.12), channel_id=1, replica_groups=mesh['uly'=32,'blk'=8] {'uly'}, dimensions={0} | all-to-all | bytes 2097152 | tf_op jit(solution)/shard_map/cond/branch_1_fun/all_to_all | solution.py:154
  103.2 0.0 collective-permute-done.1.prev_ref
  103.2 24.9 %attend.1 = bf16[32,128,128]{2,1,0:T(8,128)(2,1)S(1)} custom-call(s32[32,8]{1,0:T(8,128)S(1)} %fusion.3.list_ref, bf16[32,128,128]{2,1,0:T(8,128)(2,1)S(1)} %get-tuple-element.24.q_ref, bf16[32,256,128]{2,1,0:T(8,128)(2,1)} %collective-permute-done.1.prev_ref, bf16[32,256,128]{2,1,0:T(8,128)(2,1)S(1)} %all_to_all.20.own_ref, ...), custom_call_target="tpu_custom_call" | custom-call | tf_op jit(solution)/shard_map/attend/pallas_call | solution.py:135
  128.1 32.3 %all_to_all.21.o_ref = bf16[32,128,128]{2,1,0:T(8,128)(2,1)S(1)} all-to-all(bf16[32,128,128]{2,1,0:T(8,128)(2,1)S(1)} %attend.1), channel_id=1, replica_groups=mesh['uly'=32,'blk'=8] {'uly'}, dimensions={0} | all-to-all | bytes 2097152 | tf_op jit(solution)/shard_map/all_to_all | solution.py:154
  160.4 1.3 merge_heads.1
  (2 shorter events, 0.0 us)
Async XLA Ops:
  3.5 65.9 %copy-start = (s32[32,8]{0,1:T(8,128)S(1)}, s32[32,8]{0,1:T(8,128)}, u32[]{:S(2)}) copy-start(s32[32,8]{0,1:T(8,128)} %param.7) | copy-start | bytes 3076
  63.8 6.8 %collective-permute-start = (bf16[32,256,128]{2,1,0:T(8,128)(2,1)S(1)}, bf16[32,256,128]{2,1,0:T(8,128)(2,1)}, u32[]{:S(2)}, u32[]{:S(2)}) collective-permute-start(bf16[32,256,128]{2,1,0:T(8,128)(2,1)S(1)} %all_to_all.20.own_ref), channel_id=1, source_target_pairs={{0,1},{1,0},{2,3},{3,2},{4,5},{5,4},{6,7},{7,6},{8,9},{9,8},{10,11... | collective-permute-start | bytes 6291464 | tf_op jit(solution)/shard_map/ppermute | solution.py:164
  66.6 36.6 %collective-permute-start.1 = (bf16[32,256,128]{2,1,0:T(8,128)(2,1)S(1)}, bf16[32,256,128]{2,1,0:T(8,128)(2,1)}, u32[]{:S(2)}, u32[]{:S(2)}) collective-permute-start(bf16[32,256,128]{2,1,0:T(8,128)(2,1)S(1)} %all_to_all.20.own_ref), channel_id=1, source_target_pairs={{1,2},{2,1},{3,4},{4,3},{5,6},{6,5},{9,10},{10,9},{11,12},{12,11},... | collective-permute-start | bytes 6291464 | tf_op jit(solution)/shard_map/ppermute | solution.py:163

commit v5 on v4

--- a/solution.py
+++ b/solution.py
@@ -9,6 +9,7 @@
 PAIR = 2 * HEAD_DIM
 SPLIT_HEADS = 16
 STEP_TILES = 8
+FIRST_ROWS = 8
 
 
 def split_kernel(qkv_ref, kv_ref, q_ref):
@@ -154,6 +155,12 @@
     return lax.all_to_all(array, "uly", split_axis=0, concat_axis=0, tiled=True)
 
 
+def exchange_in_two(array):
+    first = exchange(array[:, :FIRST_ROWS])
+    array, first = lax.optimization_barrier((array, first))
+    return jnp.concatenate([first, exchange(array[:, FIRST_ROWS:])], axis=1)
+
+
 def on_device(qkv, tile_list):
     frames = lax.axis_size("blk")
     frame = lax.axis_index("blk")
@@ -162,9 +169,7 @@
     kv = exchange(kv)
     far = lax.ppermute(kv, "blk", [p for i in range(1, frames - 1, 2) for p in ((i, i + 1), (i + 1, i))])
     near = lax.ppermute(kv, "blk", [p for i in range(0, frames, 2) for p in ((i, i + 1), (i + 1, i))])
-    queries = lax.cond(odd == 0, exchange, lambda a: a, queries)
-    queries, near = lax.optimization_barrier((queries, near))
-    queries = lax.cond(odd == 1, exchange, lambda a: a, queries)
+    queries = lax.cond(odd == 0, exchange, exchange_in_two, queries)
     frame_tiles = tile_list.shape[0]
     step = tile_list // frame_tiles - frame
     slot = 1 + jnp.where(odd == 0, step, -step)

time: 164 us -> 157 us (0.957); the launches traced: 162 us -> 156 us
  blocking collectives: 125 us -> 119 us
    all_to_all x3 -> x4, blocking collectives: 125 us -> 119 us  [exchange(): return lax.all_to_all(array, 'uly', split_axis=0, concat_axis=0, tiled=True)]
  transfers between devices with their start and end apart: 2 -> 2, of which waited for: 1 -> 0; matrix products, arithmetic and copies ran while one was open for 0% -> 1% of each run, Pallas kernels for 0% -> 0%
where the time goes in v5:
time: 157 us; the launch traced here: 156 us
  blocking collectives  119 us (76%)
  Pallas kernels  30.5 us (19%)
  starting transfers between devices  5.55 us (4%)
    all_to_all x4, blocking collectives, exchange(): return lax.all_to_all(array, 'uly', split_axis=0, concat_axis=0, tiled=True)  119 us
    pallas_call x1, Pallas kernels, attend(): pl.pallas_call(attend_kernel, grid_spec=pltpu.PrefetchScalarGridSpec(num_...  25.8 us
    pallas_call x1, Pallas kernels, split_heads(): pl.pallas_call(split_kernel, grid=(heads // group,), in_specs=[pl.BlockSp...  3.46 us
  transfers between devices with their start and end apart: 2, of which 0 were waited for; matrix products, arithmetic and copies ran while one was open for 1% of the time, Pallas kernels for 0%

profile of v5, /device:TPU:37, one launch (start us, length us, event | category | flops | bytes accessed | tf_op | source)
XLA Modules:
  0.0 156.4 jit_solution(12943460586522144766)
XLA Ops:
  0.0 3.5 %split_heads.1 = (bf16[32,256,128]{2,1,0:T(8,128)(2,1)}, bf16[32,128,128]{2,1,0:T(8,128)(2,1)S(1)}) custom-call(bf16[256,6144]{1,0:T(8,128)(2,1)} %qkv_ref.1), custom_call_target="tpu_custom_call" | custom-call | tf_op jit(solution)/shard_map/split_heads/pallas_call | solution.py:32
  3.5 0.0 copy-start
  3.5 60.3 %all_to_all.25.own_ref = bf16[32,256,128]{2,1,0:T(8,128)(2,1)S(1)} all-to-all(bf16[32,256,128]{2,1,0:T(8,128)(2,1)} %get-tuple-element.15), channel_id=1, replica_groups=mesh['uly'=32,'blk'=8] {'uly'}, dimensions={0} | all-to-all | bytes 4194304 | tf_op jit(solution)/shard_map/all_to_all | solution.py:155
  63.8 2.8 %collective-permute-start.1 = (bf16[32,256,128]{2,1,0:T(8,128)(2,1)S(1)}, bf16[32,256,128]{2,1,0:T(8,128)(2,1)}, u32[]{:S(2)}, u32[]{:S(2)}) collective-permute-start(bf16[32,256,128]{2,1,0:T(8,128)(2,1)S(1)} %all_to_all.25.own_ref), channel_id=1, source_target_pairs={{0,1},{1,0},{2,3},{3,2},{4,5},{5,4},{6,7},{7,6},{8,9},{9,8},{10,11... | collective-permute-start | bytes 6291464 | tf_op jit(solution)/shard_map/ppermute | solution.py:171
  66.6 2.7 %collective-permute-start = (bf16[32,256,128]{2,1,0:T(8,128)(2,1)S(1)}, bf16[32,256,128]{2,1,0:T(8,128)(2,1)}, u32[]{:S(2)}, u32[]{:S(2)}) collective-permute-start(bf16[32,256,128]{2,1,0:T(8,128)(2,1)S(1)} %all_to_all.25.own_ref), channel_id=1, source_target_pairs={{1,2},{2,1},{3,4},{4,3},{5,6},{6,5},{9,10},{10,9},{11,12},{12,11},... | collective-permute-start | bytes 6291464 | tf_op jit(solution)/shard_map/ppermute | solution.py:170
  69.4 0.0 copy-done
  69.4 0.1 copy.3
  69.4 37.1 %conditional.1 = (bf16[32,128,128]{2,1,0:T(8,128)(2,1)}) conditional(s32[]{:T(128)} %convert_element_type.3, bf16[32,128,128]{2,1,0:T(8,128)(2,1)S(1)} %get-tuple-element.14, bf16[32,128,128]{2,1,0:T(8,128)(2,1)S(1)} %get-tuple-element.14), branch_computations={%region_0.1_spmd, %region_1.2_spmd} | conditional | flops 2097152 | bytes 6291464 | solution.py:172
  69.5 12.7 %all_to_all.22 = bf16[32,8,128]{2,1,0:T(8,128)(2,1)S(1)} all-to-all(bf16[32,8,128]{2,1,0:T(8,128)(2,1)S(1)} %slice.4), channel_id=1, replica_groups=mesh['uly'=32,'blk'=8] {'uly'}, dimensions={0} | all-to-all | bytes 131072 | tf_op jit(solution)/shard_map/cond/branch_0_fun/all_to_all | solution.py:155
  82.2 0.1 slice.5
  82.3 23.2 %all_to_all.23 = bf16[32,120,128]{2,1,0:T(8,128)(2,1)S(1)} all-to-all(bf16[32,120,128]{2,1,0:T(8,128)(2,1)S(1)} %slice.5), channel_id=1, replica_groups=mesh['uly'=32,'blk'=8] {'uly'}, dimensions={0} | all-to-all | bytes 1966080 | tf_op jit(solution)/shard_map/cond/branch_0_fun/all_to_all | solution.py:155
  105.4 1.1 pad_maximum_fusion
  106.6 0.0 collective-permute-done.1.next_ref
  106.6 0.0 collective-permute-done.prev_ref
  106.6 25.8 %attend.1 = bf16[32,128,128]{2,1,0:T(8,128)(2,1)S(1)} custom-call(s32[32,8]{1,0:T(8,128)S(1)} %fusion.3.list_ref, bf16[32,128,128]{2,1,0:T(8,128)(2,1)} %get-tuple-element.16.q_ref, bf16[32,256,128]{2,1,0:T(8,128)(2,1)} %collective-permute-done.prev_ref, bf16[32,256,128]{2,1,0:T(8,128)(2,1)S(1)} %all_to_all.25.own_ref, ...), custom_call_target="tpu_custom_call" | custom-call | tf_op jit(solution)/shard_map/attend/pallas_call | solution.py:136
  132.5 22.6 %all_to_all.26.o_ref = bf16[32,128,128]{2,1,0:T(8,128)(2,1)S(1)} all-to-all(bf16[32,128,128]{2,1,0:T(8,128)(2,1)S(1)} %attend.1), channel_id=1, replica_groups=mesh['uly'=32,'blk'=8] {'uly'}, dimensions={0} | all-to-all | bytes 2097152 | tf_op jit(solution)/shard_map/all_to_all | solution.py:155
  155.1 1.3 merge_heads.1
  (2 shorter events, 0.0 us)
Async XLA Ops:
  3.5 65.9 %copy-start = (s32[32,8]{0,1:T(8,128)S(1)}, s32[32,8]{0,1:T(8,128)}, u32[]{:S(2)}) copy-start(s32[32,8]{0,1:T(8,128)} %param.5) | copy-start | bytes 3076
  63.8 42.8 %collective-permute-start.1 = (bf16[32,256,128]{2,1,0:T(8,128)(2,1)S(1)}, bf16[32,256,128]{2,1,0:T(8,128)(2,1)}, u32[]{:S(2)}, u32[]{:S(2)}) collective-permute-start(bf16[32,256,128]{2,1,0:T(8,128)(2,1)S(1)} %all_to_all.25.own_ref), channel_id=1, source_target_pairs={{0,1},{1,0},{2,3},{3,2},{4,5},{5,4},{6,7},{7,6},{8,9},{9,8},{10,11... | collective-permute-start | bytes 6291464 | tf_op jit(solution)/shard_map/ppermute | solution.py:171
  66.6 40.0 %collective-permute-start = (bf16[32,256,128]{2,1,0:T(8,128)(2,1)S(1)}, bf16[32,256,128]{2,1,0:T(8,128)(2,1)}, u32[]{:S(2)}, u32[]{:S(2)}) collective-permute-start(bf16[32,256,128]{2,1,0:T(8,128)(2,1)S(1)} %all_to_all.25.own_ref), channel_id=1, source_target_pairs={{1,2},{2,1},{3,4},{4,3},{5,6},{6,5},{9,10},{10,9},{11,12},{12,11},... | collective-permute-start | bytes 6291464 | tf_op jit(solution)/shard_map/ppermute | solution.py:170

commit v6 on v4

--- a/solution.py
+++ b/solution.py
@@ -8,7 +8,8 @@
 HEAD_DIM = 64
 PAIR = 2 * HEAD_DIM
 SPLIT_HEADS = 16
-STEP_TILES = 8
+STEP_TILES = 16
+Z_DEVICES = 8
 
 
 def split_kernel(qkv_ref, kv_ref, q_ref):
@@ -68,36 +69,39 @@
     )(parts)
 
 
-def load_window(srcs, raw, sems):
-    tiles = srcs[0].shape[0]
-    copies = [
-        pltpu.make_async_copy(src, raw.at[pl.ds(i * tiles, tiles)], sems.at[i])
-        for i, src in enumerate(srcs)
-    ]
+def load_all(pairs, sems):
+    copies = [pltpu.make_async_copy(src, dst, sems.at[i]) for i, (src, dst) in enumerate(pairs)]
     for copy in copies:
         copy.start()
     for copy in copies:
         copy.wait()
 
 
-def padded_query(q_ref):
-    packed = q_ref * jnp.bfloat16(HEAD_DIM**-0.5)
+def padded_query(packed):
+    packed = packed * jnp.bfloat16(HEAD_DIM**-0.5)
     stacked = jnp.concatenate([packed[:, :HEAD_DIM], packed[:, HEAD_DIM:]], axis=0)
     return jnp.concatenate([stacked, jnp.zeros_like(stacked)], axis=1)
 
 
-def attend_kernel(list_ref, q_ref, prev_ref, own_ref, next_ref, o_ref, raw, sems):
+def attend_kernel(list_ref, q_ref, prev_ref, own_ref, next_ref, o_ref, asked, raw, sems):
     step = pl.program_id(0)
 
     @pl.when(step == 0)
     def _():
-        load_window((prev_ref, own_ref, next_ref), raw, sems)
-
-    count = list_ref.shape[1]
+        tiles = own_ref.shape[0]
+        pairs = [
+            (src, raw.at[pl.ds(i * tiles, tiles)])
+            for i, src in enumerate((prev_ref, own_ref, next_ref))
+        ]
+        pairs.append((q_ref, asked))
+        load_all(pairs, sems)
+
+    count = list_ref.shape[1] - 1
 
     def score(u):
-        query = padded_query(q_ref[u])
-        listed = [list_ref[step * q_ref.shape[0] + u, j] for j in range(count)]
+        tile = step * o_ref.shape[0] + u
+        query = padded_query(asked[list_ref[tile, count]])
+        listed = [list_ref[tile, j] for j in range(count)]
         dims = (((1,), (1,)), ((), ()))
         scores = [
             lax.dot_general(query, raw[t], dims, preferred_element_type=jnp.float32) for t in listed
@@ -122,8 +126,8 @@
         o_ref[u] = jnp.concatenate([out[:half], out[half:]], axis=1)
 
     held = score(0)
-    for u in range(q_ref.shape[0]):
-        following = score(u + 1) if u + 1 < q_ref.shape[0] else None
+    for u in range(o_ref.shape[0]):
+        following = score(u + 1) if u + 1 < o_ref.shape[0] else None
         finish(u, *held)
         held = following
 
@@ -137,21 +141,31 @@
         grid_spec=pltpu.PrefetchScalarGridSpec(
             num_scalar_prefetch=1,
             grid=(tiles // STEP_TILES,),
-            in_specs=[pl.BlockSpec((STEP_TILES, half, PAIR), lambda i, _: (i, 0, 0)), hbm, hbm, hbm],
+            in_specs=[hbm] * 4,
             out_specs=pl.BlockSpec((STEP_TILES, half, PAIR), lambda i, _: (i, 0, 0)),
             scratch_shapes=[
+                pltpu.VMEM((tiles, half, PAIR), jnp.bfloat16),
                 pltpu.VMEM((3 * tiles, tile_len, PAIR), jnp.bfloat16),
-                pltpu.SemaphoreType.DMA((3,)),
+                pltpu.SemaphoreType.DMA((4,)),
             ],
         ),
-        out_shape=jax.ShapeDtypeStruct(queries.shape, queries.dtype),
+        out_shape=jax.ShapeDtypeStruct((tiles, half, PAIR), queries.dtype),
         compiler_params=pltpu.CompilerParams(vmem_limit_bytes=32 * 2**20),
         name="attend",
     )(local_list, queries, before, own, after)
 
 
 def exchange(array):
-    return lax.all_to_all(array, "uly", split_axis=0, concat_axis=0, tiled=True)
+    return lax.all_to_all(array, ("y", "z"), split_axis=0, concat_axis=0, tiled=True)
+
+
+def exchange_by_axis(array):
+    y, z = lax.axis_size("y"), lax.axis_size("z")
+    parts = array.reshape((y, z) + array.shape[1:])
+    parts = lax.all_to_all(parts, "y", split_axis=0, concat_axis=0, tiled=True)
+    parts = jnp.swapaxes(parts, 0, 1)
+    parts = lax.all_to_all(parts, "z", split_axis=0, concat_axis=0, tiled=True)
+    return parts.reshape(array.shape)
 
 
 def on_device(qkv, tile_list):
@@ -162,20 +176,26 @@
     kv = exchange(kv)
     far = lax.ppermute(kv, "blk", [p for i in range(1, frames - 1, 2) for p in ((i, i + 1), (i + 1, i))])
     near = lax.ppermute(kv, "blk", [p for i in range(0, frames, 2) for p in ((i, i + 1), (i + 1, i))])
-    queries = lax.cond(odd == 0, exchange, lambda a: a, queries)
-    queries, near = lax.optimization_barrier((queries, near))
-    queries = lax.cond(odd == 1, exchange, lambda a: a, queries)
     frame_tiles = tile_list.shape[0]
     step = tile_list // frame_tiles - frame
-    slot = 1 + jnp.where(odd == 0, step, -step)
-    local_list = slot * frame_tiles + tile_list % frame_tiles
-    result = attend(local_list, queries, far, kv, near)
+    slot = 1 - jnp.where(odd == 0, step, -step)
+    listed = slot * frame_tiles + tile_list % frame_tiles
+    tiles = lax.broadcasted_iota(jnp.int32, (frame_tiles, 1), 0)
+    y, z = lax.axis_size("y"), lax.axis_size("z")
+    order = jnp.where(odd == 0, tiles, tiles % z * y + tiles // z)
+    local_list = jnp.concatenate([listed, order], axis=1)
+    queries, local_list = lax.optimization_barrier((queries, local_list))
+    queries = lax.cond(odd == 0, exchange, exchange_by_axis, queries)
+    result = attend(local_list, queries, near, kv, far)
     return merge_heads(exchange(result))
 
 
 def solution(mesh):
-    in_specs = (P(("blk", "uly"), None), P("blk", None))
-    out_specs = P(("blk", "uly"), None)
+    ring = Z_DEVICES
+    axes = mesh.devices.reshape(mesh.devices.shape[0] // ring, ring, mesh.devices.shape[1])
+    mesh = jax.sharding.Mesh(axes, ("y", "z", "blk"))
+    in_specs = (P(("blk", "y", "z"), None), P("blk", None))
+    out_specs = P(("blk", "y", "z"), None)
     return jax.shard_map(
         on_device, mesh=mesh, in_specs=in_specs, out_specs=out_specs, check_vma=False
     )

time: 164 us -> 156 us (0.951); the launches traced: 162 us -> 156 us
  blocking collectives: 125 us -> 120 us
    all_to_all x3 -> x4, blocking collectives: 125 us -> 120 us  [the longest x2 86.3 us: exchange(): lax.all_to_all(array, ('y', 'z'), split_axis=0, concat_axis=0, tiled=True)]
    ppermute x1, starting transfers between devices: 2.7 us -> 5.55 us  [on_device(): lax.ppermute(kv, 'blk', [p for i in range(1, frames - 1, 2) for p in ((i,...]
    ppermute x1, starting transfers between devices: 2.85 us -> 0.09 us  [on_device(): lax.ppermute(kv, 'blk', [p for i in range(0, frames, 2) for p in ((i, i +...]
  transfers between devices with their start and end apart: 2 -> 2, of which waited for: 1 -> 0; matrix products, arithmetic and copies ran while one was open for 0% -> 0% of each run, Pallas kernels for 0% -> 0%
where the time goes in v6:
time: 156 us
  blocking collectives  120 us (77%)
  Pallas kernels  29.4 us (19%)
  starting transfers between devices  5.64 us (4%)
    all_to_all x2, blocking collectives, exchange(): lax.all_to_all(array, ('y', 'z'), split_axis=0, concat_axis=0, tiled=True)  86.3 us
    pallas_call x1, Pallas kernels, attend(): pl.pallas_call(attend_kernel, grid_spec=pltpu.PrefetchScalarGridSpec(num_...  24.6 us
    all_to_all x1, blocking collectives, exchange_by_axis(): parts = lax.all_to_all(parts, 'z', split_axis=0, concat_axis=0, tiled=True)  19.4 us
    all_to_all x1, blocking collectives, exchange_by_axis(): parts = lax.all_to_all(parts, 'y', split_axis=0, concat_axis=0, tiled=True)  14.6 us
    ppermute x1, starting transfers between devices, on_device(): lax.ppermute(kv, 'blk', [p for i in range(1, frames - 1, 2) for p in ((i,...  5.55 us
    pallas_call x1, Pallas kernels, split_heads(): pl.pallas_call(split_kernel, grid=(heads // group,), in_specs=[pl.BlockSp...  3.46 us
  transfers between devices with their start and end apart: 2, of which 0 were waited for; matrix products, arithmetic and copies ran while one was open for 0% of the time, Pallas kernels for 0%

profile of v6, /device:TPU:37, one launch (start us, length us, event | category | flops | bytes accessed | tf_op | source)
XLA Modules:
  0.0 155.7 jit_solution(4891784475400024852)
XLA Ops:
  0.0 3.5 %split_heads.1 = (bf16[32,256,128]{2,1,0:T(8,128)(2,1)}, bf16[32,128,128]{2,1,0:T(8,128)(2,1)S(1)}) custom-call(bf16[256,6144]{1,0:T(8,128)(2,1)} %qkv_ref.1), custom_call_target="tpu_custom_call" | custom-call | tf_op jit(solution)/shard_map/split_heads/pallas_call | solution.py:32
  3.5 0.0 copy-start
  3.5 60.3 %all_to_all.25.own_ref = bf16[32,256,128]{2,1,0:T(8,128)(2,1)S(1)} all-to-all(bf16[32,256,128]{2,1,0:T(8,128)(2,1)} %get-tuple-element.17), channel_id=1, replica_groups=mesh['y'=4,'z'=8,'blk'=8] {'y','z'}, dimensions={0} | all-to-all | bytes 4194304 | tf_op jit(solution)/shard_map/all_to_all | solution.py:159
  63.8 5.5 %collective-permute-start.1 = (bf16[32,256,128]{2,1,0:T(8,128)(2,1)S(1)}, bf16[32,256,128]{2,1,0:T(8,128)(2,1)}, u32[]{:S(2)}, u32[]{:S(2)}) collective-permute-start(bf16[32,256,128]{2,1,0:T(8,128)(2,1)S(1)} %all_to_all.25.own_ref), channel_id=1, source_target_pairs={{1,2},{2,1},{3,4},{4,3},{5,6},{6,5},{9,10},{10,9},{11,12},{12,11},... | collective-permute-start | bytes 6291464 | tf_op jit(solution)/shard_map/ppermute | solution.py:177
  69.3 0.1 collective-permute-start
  69.4 0.0 copy-done
  69.5 0.1 copy.13
  69.6 0.1 pad_add_fusion.list_ref
  69.7 34.1 %conditional.1 = (bf16[32,128,128]{2,1,0:T(8,128)(2,1)}) conditional(s32[]{:T(128)} %convert_element_type.3, bf16[32,128,128]{2,1,0:T(8,128)(2,1)S(1)} %get-tuple-element.16, bf16[32,128,128]{2,1,0:T(8,128)(2,1)S(1)} %get-tuple-element.16), branch_computations={%region_0.1_spmd, %region_1.2_spmd} | conditional | bytes 6291464 | solution.py:188
  69.7 14.6 %all_to_all.22 = bf16[4,8,128,128]{3,2,1,0:T(8,128)(2,1)S(1)} all-to-all(bf16[4,8,128,128]{3,2,1,0:T(8,128)(2,1)S(1)} %bitcast.5), channel_id=1, replica_groups=mesh['y'=4,'z'=8,'blk'=8] {'y'}, dimensions={0} | all-to-all | bytes 2097152 | tf_op jit(solution)/shard_map/cond/branch_0_fun/all_to_all | solution.py:165
  84.3 0.1 copy.18
  84.3 19.4 %all_to_all.23 = bf16[8,4,128,128]{3,2,1,0:T(8,128)(2,1)} all-to-all(bf16[8,4,128,128]{3,2,1,0:T(8,128)(2,1)S(1)} %bitcast.6), channel_id=1, replica_groups=mesh['y'=4,'z'=8,'blk'=8] {'z'}, dimensions={0} | all-to-all | bytes 2097152 | tf_op jit(solution)/shard_map/cond/branch_0_fun/all_to_all | solution.py:167
  103.7 0.0 collective-permute-done.1.next_ref
  103.7 0.0 collective-permute-done.prev_ref
  103.8 24.6 %attend.1 = bf16[32,128,128]{2,1,0:T(8,128)(2,1)S(1)} custom-call(s32[32,9]{1,0:T(8,128)S(1)} %pad_add_fusion.list_ref, bf16[32,128,128]{2,1,0:T(8,128)(2,1)} %get-tuple-element.18.q_ref, bf16[32,256,128]{2,1,0:T(8,128)(2,1)} %collective-permute-done.prev_ref, bf16[32,256,128]{2,1,0:T(8,128)(2,1)S(1)} %all_to_all.25.own_ref, ...), custom_call_target="tpu_custom_call" | custom-call | tf_op jit(solution)/shard_map/attend/pallas_call | solution.py:139
  128.4 26.0 %all_to_all.26.o_ref = bf16[32,128,128]{2,1,0:T(8,128)(2,1)S(1)} all-to-all(bf16[32,128,128]{2,1,0:T(8,128)(2,1)S(1)} %attend.1), channel_id=1, replica_groups=mesh['y'=4,'z'=8,'blk'=8] {'y','z'}, dimensions={0} | all-to-all | bytes 2097152 | tf_op jit(solution)/shard_map/all_to_all | solution.py:159
  154.4 1.3 merge_heads.1
  (2 shorter events, 0.0 us)
Async XLA Ops:
  3.5 66.0 %copy-start = (s32[32,8]{0,1:T(8,128)S(1)}, s32[32,8]{0,1:T(8,128)}, u32[]{:S(2)}) copy-start(s32[32,8]{0,1:T(8,128)} %param.5) | copy-start | bytes 3076
  63.8 40.0 %collective-permute-start.1 = (bf16[32,256,128]{2,1,0:T(8,128)(2,1)S(1)}, bf16[32,256,128]{2,1,0:T(8,128)(2,1)}, u32[]{:S(2)}, u32[]{:S(2)}) collective-permute-start(bf16[32,256,128]{2,1,0:T(8,128)(2,1)S(1)} %all_to_all.25.own_ref), channel_id=1, source_target_pairs={{1,2},{2,1},{3,4},{4,3},{5,6},{6,5},{9,10},{10,9},{11,12},{12,11},... | collective-permute-start | bytes 6291464 | tf_op jit(solution)/shard_map/ppermute | solution.py:177
  69.3 34.4 %collective-permute-start = (bf16[32,256,128]{2,1,0:T(8,128)(2,1)S(1)}, bf16[32,256,128]{2,1,0:T(8,128)(2,1)}, u32[]{:S(2)}, u32[]{:S(2)}) collective-permute-start(bf16[32,256,128]{2,1,0:T(8,128)(2,1)S(1)} %all_to_all.25.own_ref), channel_id=1, source_target_pairs={{0,1},{1,0},{2,3},{3,2},{4,5},{5,4},{6,7},{7,6},{8,9},{9,8},{10,11... | collective-permute-start | bytes 6291464 | tf_op jit(solution)/shard_map/ppermute | solution.py:178

commit v7 on v6

--- a/solution.py
+++ b/solution.py
@@ -96,11 +96,11 @@
         pairs.append((q_ref, asked))
         load_all(pairs, sems)
 
-    count = list_ref.shape[1] - 1
+    count = list_ref.shape[1]
 
     def score(u):
         tile = step * o_ref.shape[0] + u
-        query = padded_query(asked[list_ref[tile, count]])
+        query = padded_query(asked[tile])
         listed = [list_ref[tile, j] for j in range(count)]
         dims = (((1,), (1,)), ((), ()))
         scores = [
@@ -168,24 +168,26 @@
     return parts.reshape(array.shape)
 
 
+def late_frame(frame):
+    return (frame + 1) // 2 % 2
+
+
 def on_device(qkv, tile_list):
     frames = lax.axis_size("blk")
     frame = lax.axis_index("blk")
-    odd = frame % 2
     kv, queries = split_heads(qkv)
-    kv = exchange(kv)
+    kv = lax.cond(late_frame(frame) == 0, exchange, exchange_by_axis, kv)
     far = lax.ppermute(kv, "blk", [p for i in range(1, frames - 1, 2) for p in ((i, i + 1), (i + 1, i))])
+    queries = exchange(queries)
     near = lax.ppermute(kv, "blk", [p for i in range(0, frames, 2) for p in ((i, i + 1), (i + 1, i))])
+    far, queries, tile_list = lax.optimization_barrier((far, queries, tile_list))
     frame_tiles = tile_list.shape[0]
-    step = tile_list // frame_tiles - frame
-    slot = 1 - jnp.where(odd == 0, step, -step)
-    listed = slot * frame_tiles + tile_list % frame_tiles
-    tiles = lax.broadcasted_iota(jnp.int32, (frame_tiles, 1), 0)
+    their_frame, place = tile_list // frame_tiles, tile_list % frame_tiles
+    step = their_frame - frame
+    slot = 1 - jnp.where(frame % 2 == 0, step, -step)
     y, z = lax.axis_size("y"), lax.axis_size("z")
-    order = jnp.where(odd == 0, tiles, tiles % z * y + tiles // z)
-    local_list = jnp.concatenate([listed, order], axis=1)
-    queries, local_list = lax.optimization_barrier((queries, local_list))
-    queries = lax.cond(odd == 0, exchange, exchange_by_axis, queries)
+    place = jnp.where(late_frame(their_frame) == 0, place, place % z * y + place // z)
+    local_list = slot * frame_tiles + place
     result = attend(local_list, queries, near, kv, far)
     return merge_heads(exchange(result))
 

time: 156 us -> 160 us (1.026)
  blocking collectives: 120 us -> 91.6 us
  waiting for transfers between devices: 0.01 us -> 18.8 us
  starting transfers between devices: 5.64 us -> 19.9 us
    all_to_all x2 -> x1, blocking collectives: 86.3 us -> 24.6 us  [exchange(): lax.all_to_all(array, ('y', 'z'), split_axis=0, concat_axis=0, tiled=True)]
    all_to_all x1, blocking collectives: 19.4 us -> 42.3 us  [exchange_by_axis(): parts = lax.all_to_all(parts, 'z', split_axis=0, concat_axis=0, tiled=True)]
    all_to_all x0 -> x1, waiting for transfers between devices: none -> 17.7 us  [exchange(): lax.all_to_all(array, ('y', 'z'), split_axis=0, concat_axis=0, tiled=True)]
    all_to_all x1, blocking collectives: 14.6 us -> 24.7 us  [exchange_by_axis(): parts = lax.all_to_all(parts, 'y', split_axis=0, concat_axis=0, tiled=True)]
    ppermute x1, starting transfers between devices: 5.55 us -> 14.8 us  [on_device(): lax.ppermute(kv, 'blk', [p for i in range(1, frames - 1, 2) for p in ((i,...]
    all_to_all x0 -> x1, starting transfers between devices: none -> 4.78 us  [exchange(): lax.all_to_all(array, ('y', 'z'), split_axis=0, concat_axis=0, tiled=True)]
  transfers between devices with their start and end apart: 2 -> 3, of which waited for: 0 -> 2; matrix products, arithmetic and copies ran while one was open for 0% -> 0% of each run, Pallas kernels for 0% -> 0%
where the time goes in v7:
time: 160 us
  blocking collectives  91.6 us (57%)
  Pallas kernels  28.8 us (18%)
  starting transfers between devices  19.9 us (12%)
  waiting for transfers between devices  18.8 us (12%)
    all_to_all x1, blocking collectives, exchange_by_axis(): parts = lax.all_to_all(parts, 'z', split_axis=0, concat_axis=0, tiled=True)  42.3 us
    all_to_all x1, blocking collectives, exchange_by_axis(): parts = lax.all_to_all(parts, 'y', split_axis=0, concat_axis=0, tiled=True)  24.7 us
    all_to_all x1, blocking collectives, exchange(): lax.all_to_all(array, ('y', 'z'), split_axis=0, concat_axis=0, tiled=True)  24.6 us
    pallas_call x1, Pallas kernels, attend(): pl.pallas_call(attend_kernel, grid_spec=pltpu.PrefetchScalarGridSpec(num_...  24.3 us
    all_to_all x1, waiting for transfers between devices, exchange(): lax.all_to_all(array, ('y', 'z'), split_axis=0, concat_axis=0, tiled=True)  17.7 us
    ppermute x1, starting transfers between devices, on_device(): lax.ppermute(kv, 'blk', [p for i in range(1, frames - 1, 2) for p in ((i,...  14.8 us
    all_to_all x1, starting transfers between devices, exchange(): lax.all_to_all(array, ('y', 'z'), split_axis=0, concat_axis=0, tiled=True)  4.78 us
    pallas_call x1, Pallas kernels, split_heads(): pl.pallas_call(split_kernel, grid=(heads // group,), in_specs=[pl.BlockSp...  3.31 us
  transfers between devices with their start and end apart: 3, of which 2 were waited for; matrix products, arithmetic and copies ran while one was open for 0% of the time, Pallas kernels for 0%

profile of v7, /device:TPU:37, one launch (start us, length us, event | category | flops | bytes accessed | tf_op | source)
XLA Modules:
  0.0 159.5 jit_solution(15226826359682471445)
XLA Ops:
  0.0 3.3 %split_heads.1 = (bf16[32,256,128]{2,1,0:T(8,128)(2,1)S(1)}, bf16[32,128,128]{2,1,0:T(8,128)(2,1)}) custom-call(bf16[256,6144]{1,0:T(8,128)(2,1)} %qkv_ref.1), custom_call_target="tpu_custom_call" | custom-call | tf_op jit(solution)/shard_map/split_heads/pallas_call | solution.py:32
  3.3 67.2 %conditional.1 = (bf16[32,256,128]{2,1,0:T(8,128)(2,1)}) conditional(s32[]{:T(128)} %convert_element_type.3, bf16[32,256,128]{2,1,0:T(8,128)(2,1)S(1)} %get-tuple-element.15, bf16[32,256,128]{2,1,0:T(8,128)(2,1)S(1)} %get-tuple-element.15), branch_computations={%region_0.1_spmd, %region_1.2_spmd} | conditional | bytes 12582920 | solution.py:179
  3.3 24.7 %all_to_all.22 = bf16[4,8,256,128]{3,2,1,0:T(8,128)(2,1)S(1)} all-to-all(bf16[4,8,256,128]{3,2,1,0:T(8,128)(2,1)S(1)} %bitcast.5), channel_id=1, replica_groups=mesh['y'=4,'z'=8,'blk'=8] {'y'}, dimensions={0} | all-to-all | bytes 4194304 | tf_op jit(solution)/shard_map/cond/branch_0_fun/all_to_all | solution.py:165
  28.1 0.2 copy.18
  28.3 42.3 %all_to_all.23 = bf16[8,4,256,128]{3,2,1,0:T(8,128)(2,1)} all-to-all(bf16[8,4,256,128]{3,2,1,0:T(8,128)(2,1)S(1)} %bitcast.6), channel_id=1, replica_groups=mesh['y'=4,'z'=8,'blk'=8] {'z'}, dimensions={0} | all-to-all | bytes 4194304 | tf_op jit(solution)/shard_map/cond/branch_0_fun/all_to_all | solution.py:167
  70.5 0.0 copy-start
  70.5 14.8 %collective-permute-start = (bf16[32,256,128]{2,1,0:T(8,128)(2,1)}, bf16[32,256,128]{2,1,0:T(8,128)(2,1)S(1)}, u32[]{:S(2)}, u32[]{:S(2)}) collective-permute-start(bf16[32,256,128]{2,1,0:T(8,128)(2,1)} %get-tuple-element.20.own_ref), channel_id=1, source_target_pairs={{1,2},{2,1},{3,4},{4,3},{5,6},{6,5},{9,10},{10,9},{11,12},{12,11},... | collective-permute-start | bytes 6291464 | tf_op jit(solution)/shard_map/ppermute | solution.py:180
  85.3 4.8 %all-to-all-start.3 = ((bf16[32,128,128]{2,1,0:T(8,128)(2,1)}), bf16[32,128,128]{2,1,0:T(8,128)(2,1)S(1)}, u32[]{:S(2)}, u32[]{:S(2)}) async-start(bf16[32,128,128]{2,1,0:T(8,128)(2,1)} %get-tuple-element.16), calls=%async_computation.3 | async-start | bytes 2097152 | tf_op jit(solution)/shard_map/all_to_all | solution.py:159
  90.1 0.3 collective-permute-start.1
  90.4 17.7 %all-to-all-done.3.q_ref = bf16[32,128,128]{2,1,0:T(8,128)(2,1)S(1)} async-done(((bf16[32,128,128]{2,1,0:T(8,128)(2,1)}), bf16[32,128,128]{2,1,0:T(8,128)(2,1)S(1)}, u32[]{:S(2)}, u32[]{:S(2)}) %all-to-all-start.3) | async-done | bytes 1048608 | tf_op jit(solution)/shard_map/all_to_all | solution.py:159
  108.1 1.2 collective-permute-done.next_ref
  109.3 0.0 copy-done
  109.3 0.1 copy.13
  109.3 0.1 fusion.2.list_ref
  109.4 0.0 collective-permute-done.1.prev_ref
  109.4 24.3 %attend.1 = bf16[32,128,128]{2,1,0:T(8,128)(2,1)S(1)} custom-call(s32[32,8]{1,0:T(8,128)S(1)} %fusion.2.list_ref, bf16[32,128,128]{2,1,0:T(8,128)(2,1)S(1)} %all-to-all-done.3.q_ref, bf16[32,256,128]{2,1,0:T(8,128)(2,1)} %collective-permute-done.1.prev_ref, bf16[32,256,128]{2,1,0:T(8,128)(2,1)} %get-tuple-element.20.own_ref, ...), custom_call_target="tpu_custom_call" | custom-call | tf_op jit(solution)/shard_map/attend/pallas_call | solution.py:139
  133.7 24.6 %all_to_all.25.o_ref = bf16[32,128,128]{2,1,0:T(8,128)(2,1)S(1)} all-to-all(bf16[32,128,128]{2,1,0:T(8,128)(2,1)S(1)} %attend.1), channel_id=1, replica_groups=mesh['y'=4,'z'=8,'blk'=8] {'y','z'}, dimensions={0} | all-to-all | bytes 2097152 | tf_op jit(solution)/shard_map/all_to_all | solution.py:159
  158.3 1.3 merge_heads.1
Async XLA Ops:
  70.5 38.7 %copy-start = (s32[32,8]{0,1:T(8,128)S(1)}, s32[32,8]{0,1:T(8,128)}, u32[]{:S(2)}) copy-start(s32[32,8]{0,1:T(8,128)} %param.5) | copy-start | bytes 3076
  70.5 38.7 %collective-permute-start = (bf16[32,256,128]{2,1,0:T(8,128)(2,1)}, bf16[32,256,128]{2,1,0:T(8,128)(2,1)S(1)}, u32[]{:S(2)}, u32[]{:S(2)}) collective-permute-start(bf16[32,256,128]{2,1,0:T(8,128)(2,1)} %get-tuple-element.20.own_ref), channel_id=1, source_target_pairs={{1,2},{2,1},{3,4},{4,3},{5,6},{6,5},{9,10},{10,9},{11,12},{12,11},... | collective-permute-start | bytes 6291464 | tf_op jit(solution)/shard_map/ppermute | solution.py:180
  85.3 22.7 %all-to-all-start.3 = ((bf16[32,128,128]{2,1,0:T(8,128)(2,1)}), bf16[32,128,128]{2,1,0:T(8,128)(2,1)S(1)}, u32[]{:S(2)}, u32[]{:S(2)}) async-start(bf16[32,128,128]{2,1,0:T(8,128)(2,1)} %get-tuple-element.16), calls=%async_computation.3 | async-start | bytes 2097152 | tf_op jit(solution)/shard_map/all_to_all | solution.py:159
  90.1 19.3 %collective-permute-start.1 = (bf16[32,256,128]{2,1,0:T(8,128)(2,1)}, bf16[32,256,128]{2,1,0:T(8,128)(2,1)}, u32[]{:S(2)}, u32[]{:S(2)}) collective-permute-start(bf16[32,256,128]{2,1,0:T(8,128)(2,1)} %get-tuple-element.20.own_ref), channel_id=1, source_target_pairs={{0,1},{1,0},{2,3},{3,2},{4,5},{5,4},{6,7},{7,6},{8,9},{9,8},{10,11... | collective-permute-start | bytes 6291464 | tf_op jit(solution)/shard_map/ppermute | solution.py:182

commit v8 on v7

--- a/solution.py
+++ b/solution.py
@@ -9,7 +9,7 @@
 PAIR = 2 * HEAD_DIM
 SPLIT_HEADS = 16
 STEP_TILES = 16
-Z_DEVICES = 8
+FIRST_ROWS = 8
 
 
 def split_kernel(qkv_ref, kv_ref, q_ref):
@@ -156,16 +156,13 @@
 
 
 def exchange(array):
-    return lax.all_to_all(array, ("y", "z"), split_axis=0, concat_axis=0, tiled=True)
+    return lax.all_to_all(array, "uly", split_axis=0, concat_axis=0, tiled=True)
 
 
-def exchange_by_axis(array):
-    y, z = lax.axis_size("y"), lax.axis_size("z")
-    parts = array.reshape((y, z) + array.shape[1:])
-    parts = lax.all_to_all(parts, "y", split_axis=0, concat_axis=0, tiled=True)
-    parts = jnp.swapaxes(parts, 0, 1)
-    parts = lax.all_to_all(parts, "z", split_axis=0, concat_axis=0, tiled=True)
-    return parts.reshape(array.shape)
+def exchange_in_two(array):
+    first = exchange(array[:, :FIRST_ROWS])
+    array, first = lax.optimization_barrier((array, first))
+    return jnp.concatenate([first, exchange(array[:, FIRST_ROWS:])], axis=1)
 
 
 def late_frame(frame):
@@ -176,7 +173,7 @@
     frames = lax.axis_size("blk")
     frame = lax.axis_index("blk")
     kv, queries = split_heads(qkv)
-    kv = lax.cond(late_frame(frame) == 0, exchange, exchange_by_axis, kv)
+    kv = lax.cond(late_frame(frame) == 0, exchange, exchange_in_two, kv)
     far = lax.ppermute(kv, "blk", [p for i in range(1, frames - 1, 2) for p in ((i, i + 1), (i + 1, i))])
     queries = exchange(queries)
     near = lax.ppermute(kv, "blk", [p for i in range(0, frames, 2) for p in ((i, i + 1), (i + 1, i))])
@@ -185,19 +182,14 @@
     their_frame, place = tile_list // frame_tiles, tile_list % frame_tiles
     step = their_frame - frame
     slot = 1 - jnp.where(frame % 2 == 0, step, -step)
-    y, z = lax.axis_size("y"), lax.axis_size("z")
-    place = jnp.where(late_frame(their_frame) == 0, place, place % z * y + place // z)
     local_list = slot * frame_tiles + place
     result = attend(local_list, queries, near, kv, far)
     return merge_heads(exchange(result))
 
 
 def solution(mesh):
-    ring = Z_DEVICES
-    axes = mesh.devices.reshape(mesh.devices.shape[0] // ring, ring, mesh.devices.shape[1])
-    mesh = jax.sharding.Mesh(axes, ("y", "z", "blk"))
-    in_specs = (P(("blk", "y", "z"), None), P("blk", None))
-    out_specs = P(("blk", "y", "z"), None)
+    in_specs = (P(("blk", "uly"), None), P("blk", None))
+    out_specs = P(("blk", "uly"), None)
     return jax.shard_map(
         on_device, mesh=mesh, in_specs=in_specs, out_specs=out_specs, check_vma=False
     )

time: 160 us -> 148 us (0.925)
  starting transfers between devices: 19.9 us -> 10.9 us
  blocking collectives: 91.6 us -> 88.4 us
    ppermute x1, starting transfers between devices: 14.8 us -> 4.24 us  [on_device(): lax.ppermute(kv, 'blk', [p for i in range(1, frames - 1, 2) for p in ((i,...]
    all_to_all x3, blocking collectives: 91.6 us -> 88.4 us  [exchange(): return lax.all_to_all(array, 'uly', split_axis=0, concat_axis=0, tiled=True)]
  transfers between devices with their start and end apart: 3 -> 3, of which waited for: 2 -> 1; matrix products, arithmetic and copies ran while one was open for 0% -> 0% of each run, Pallas kernels for 0% -> 0%
where the time goes in v8:
time: 148 us
  blocking collectives  88.4 us (60%)
  Pallas kernels  28.8 us (19%)
  waiting for transfers between devices  17.6 us (12%)
  starting transfers between devices  10.9 us (7%)
  other arithmetic  1.62 us (1%)
    all_to_all x3, blocking collectives, exchange(): return lax.all_to_all(array, 'uly', split_axis=0, concat_axis=0, tiled=True)  88.4 us
    pallas_call x1, Pallas kernels, attend(): pl.pallas_call(attend_kernel, grid_spec=pltpu.PrefetchScalarGridSpec(num_...  24.3 us
    all_to_all x1, waiting for transfers between devices, exchange(): return lax.all_to_all(array, 'uly', split_axis=0, concat_axis=0, tiled=True)  17.5 us
    all_to_all x1, starting transfers between devices, exchange(): return lax.all_to_all(array, 'uly', split_axis=0, concat_axis=0, tiled=True)  6.37 us
    ppermute x1, starting transfers between devices, on_device(): lax.ppermute(kv, 'blk', [p for i in range(1, frames - 1, 2) for p in ((i,...  4.24 us
    pallas_call x1, Pallas kernels, split_heads(): pl.pallas_call(split_kernel, grid=(heads // group,), in_specs=[pl.BlockSp...  3.31 us
  transfers between devices with their start and end apart: 3, of which 1 were waited for; matrix products, arithmetic and copies ran while one was open for 0% of the time, Pallas kernels for 0%

profile of v8, /device:TPU:37, one launch (start us, length us, event | category | flops | bytes accessed | tf_op | source)
XLA Modules:
  0.0 147.6 jit_solution(16357341052711207153)
XLA Ops:
  0.0 3.3 %split_heads.1 = (bf16[32,256,128]{2,1,0:T(8,128)(2,1)S(1)}, bf16[32,128,128]{2,1,0:T(8,128)(2,1)}) custom-call(bf16[256,6144]{1,0:T(8,128)(2,1)} %qkv_ref.1), custom_call_target="tpu_custom_call" | custom-call | tf_op jit(solution)/shard_map/split_heads/pallas_call | solution.py:32
  3.3 64.4 %conditional.1 = (bf16[32,256,128]{2,1,0:T(8,128)(2,1)}) conditional(s32[]{:T(128)} %convert_element_type.3, bf16[32,256,128]{2,1,0:T(8,128)(2,1)S(1)} %get-tuple-element.17, bf16[32,256,128]{2,1,0:T(8,128)(2,1)S(1)} %get-tuple-element.17), branch_computations={%region_0.1_spmd, %region_1.2_spmd} | conditional | flops 4194304 | bytes 12582920 | solution.py:176
  3.3 19.2 %all_to_all.22 = bf16[32,8,128]{2,1,0:T(8,128)(2,1)S(1)} all-to-all(bf16[32,8,128]{2,1,0:T(8,128)(2,1)S(1)} %slice.4), channel_id=1, replica_groups=mesh['uly'=32,'blk'=8] {'uly'}, dimensions={0} | all-to-all | bytes 131072 | tf_op jit(solution)/shard_map/cond/branch_0_fun/all_to_all | solution.py:159
  22.6 0.2 slice.5
  22.7 43.4 %all_to_all.23 = bf16[32,248,128]{2,1,0:T(8,128)(2,1)S(1)} all-to-all(bf16[32,248,128]{2,1,0:T(8,128)(2,1)S(1)} %slice.5), channel_id=1, replica_groups=mesh['uly'=32,'blk'=8] {'uly'}, dimensions={0} | all-to-all | bytes 4063232 | tf_op jit(solution)/shard_map/cond/branch_0_fun/all_to_all | solution.py:159
  66.1 1.6 %pad_maximum_fusion = bf16[32,256,128]{2,1,0:T(8,128)(2,1)} fusion(bf16[32,248,128]{2,1,0:T(8,128)(2,1)S(1)} %all_to_all.23, bf16[32,8,128]{2,1,0:T(8,128)(2,1)S(1)} %all_to_all.22), kind=kLoop, calls=%fused_computation | loop fusion | flops 4194304 | bytes 4194304 | tf_op jit(solution)/shard_map/cond/branch_0_fun/concatenate | solution.py:165
  67.7 0.0 copy-start
  67.7 4.2 %collective-permute-start = (bf16[32,256,128]{2,1,0:T(8,128)(2,1)}, bf16[32,256,128]{2,1,0:T(8,128)(2,1)S(1)}, u32[]{:S(2)}, u32[]{:S(2)}) collective-permute-start(bf16[32,256,128]{2,1,0:T(8,128)(2,1)} %get-tuple-element.22.own_ref), channel_id=1, source_target_pairs={{1,2},{2,1},{3,4},{4,3},{5,6},{6,5},{9,10},{10,9},{11,12},{12,11},... | collective-permute-start | bytes 6291464 | tf_op jit(solution)/shard_map/ppermute | solution.py:177
  71.9 6.4 %all-to-all-start.3 = ((bf16[32,128,128]{2,1,0:T(8,128)(2,1)}), bf16[32,128,128]{2,1,0:T(8,128)(2,1)S(1)}, u32[]{:S(2)}, u32[]{:S(2)}) async-start(bf16[32,128,128]{2,1,0:T(8,128)(2,1)} %get-tuple-element.18), calls=%async_computation.3 | async-start | bytes 2097152 | tf_op jit(solution)/shard_map/all_to_all | solution.py:159
  78.3 0.3 collective-permute-start.1
  78.6 17.5 %all-to-all-done.3.q_ref = bf16[32,128,128]{2,1,0:T(8,128)(2,1)S(1)} async-done(((bf16[32,128,128]{2,1,0:T(8,128)(2,1)}), bf16[32,128,128]{2,1,0:T(8,128)(2,1)S(1)}, u32[]{:S(2)}, u32[]{:S(2)}) %all-to-all-start.3) | async-done | bytes 1048608 | tf_op jit(solution)/shard_map/all_to_all | solution.py:159
  96.2 0.0 collective-permute-done.next_ref
  96.2 0.0 copy-done
  96.2 0.1 copy.3
  96.3 0.0 collective-permute-done.1.prev_ref
  96.3 24.3 %attend.1 = bf16[32,128,128]{2,1,0:T(8,128)(2,1)S(1)} custom-call(s32[32,8]{1,0:T(8,128)S(1)} %fusion.3.list_ref, bf16[32,128,128]{2,1,0:T(8,128)(2,1)S(1)} %all-to-all-done.3.q_ref, bf16[32,256,128]{2,1,0:T(8,128)(2,1)} %collective-permute-done.1.prev_ref, bf16[32,256,128]{2,1,0:T(8,128)(2,1)} %get-tuple-element.22.own_ref, ...), custom_call_target="tpu_custom_call" | custom-call | tf_op jit(solution)/shard_map/attend/pallas_call | solution.py:139
  120.5 25.8 %all_to_all.25.o_ref = bf16[32,128,128]{2,1,0:T(8,128)(2,1)S(1)} all-to-all(bf16[32,128,128]{2,1,0:T(8,128)(2,1)S(1)} %attend.1), channel_id=1, replica_groups=mesh['uly'=32,'blk'=8] {'uly'}, dimensions={0} | all-to-all | bytes 2097152 | tf_op jit(solution)/shard_map/all_to_all | solution.py:159
  146.3 1.3 merge_heads.1
  (2 shorter events, 0.0 us)
Async XLA Ops:
  67.7 28.5 %copy-start = (s32[32,8]{0,1:T(8,128)S(1)}, s32[32,8]{0,1:T(8,128)}, u32[]{:S(2)}) copy-start(s32[32,8]{0,1:T(8,128)} %param.5) | copy-start | bytes 3076
  67.7 28.5 %collective-permute-start = (bf16[32,256,128]{2,1,0:T(8,128)(2,1)}, bf16[32,256,128]{2,1,0:T(8,128)(2,1)S(1)}, u32[]{:S(2)}, u32[]{:S(2)}) collective-permute-start(bf16[32,256,128]{2,1,0:T(8,128)(2,1)} %get-tuple-element.22.own_ref), channel_id=1, source_target_pairs={{1,2},{2,1},{3,4},{4,3},{5,6},{6,5},{9,10},{10,9},{11,12},{12,11},... | collective-permute-start | bytes 6291464 | tf_op jit(solution)/shard_map/ppermute | solution.py:177
  71.9 24.2 %all-to-all-start.3 = ((bf16[32,128,128]{2,1,0:T(8,128)(2,1)}), bf16[32,128,128]{2,1,0:T(8,128)(2,1)S(1)}, u32[]{:S(2)}, u32[]{:S(2)}) async-start(bf16[32,128,128]{2,1,0:T(8,128)(2,1)} %get-tuple-element.18), calls=%async_computation.3 | async-start | bytes 2097152 | tf_op jit(solution)/shard_map/all_to_all | solution.py:159
  78.3 18.0 %collective-permute-start.1 = (bf16[32,256,128]{2,1,0:T(8,128)(2,1)}, bf16[32,256,128]{2,1,0:T(8,128)(2,1)}, u32[]{:S(2)}, u32[]{:S(2)}) collective-permute-start(bf16[32,256,128]{2,1,0:T(8,128)(2,1)} %get-tuple-element.22.own_ref), channel_id=1, source_target_pairs={{0,1},{1,0},{2,3},{3,2},{4,5},{5,4},{6,7},{7,6},{8,9},{9,8},{10,11... | collective-permute-start | bytes 6291464 | tf_op jit(solution)/shard_map/ppermute | solution.py:179

commit v9 on v8

--- a/solution.py
+++ b/solution.py
@@ -12,7 +12,7 @@
 FIRST_ROWS = 8
 
 
-def split_kernel(qkv_ref, kv_ref, q_ref):
+def split_kernel(qkv_ref, kv_ref, first_ref, rest_ref):
     half = qkv_ref.shape[0] // 2
     for pair in range(kv_ref.shape[0] // 2):
         base = pair * 6 * HEAD_DIM
@@ -20,9 +20,11 @@
             col = base + odd * 3 * HEAD_DIM
             head = 2 * pair + odd
             kv_ref[head] = qkv_ref[:, col + HEAD_DIM : col + 3 * HEAD_DIM]
-            q_ref[head] = jnp.concatenate(
+            packed = jnp.concatenate(
                 [qkv_ref[:half, col : col + HEAD_DIM], qkv_ref[half:, col : col + HEAD_DIM]], axis=1
             )
+            first_ref[head] = packed[:FIRST_ROWS]
+            rest_ref[head] = packed[FIRST_ROWS:]
 
 
 def split_heads(qkv):
@@ -35,11 +37,13 @@
         in_specs=[pl.BlockSpec((tokens, group * 3 * HEAD_DIM), lambda i: (0, i))],
         out_specs=[
             pl.BlockSpec((group, tokens, PAIR), lambda i: (i, 0, 0)),
-            pl.BlockSpec((group, tokens // 2, PAIR), lambda i: (i, 0, 0)),
+            pl.BlockSpec((group, FIRST_ROWS, PAIR), lambda i: (i, 0, 0)),
+            pl.BlockSpec((group, tokens // 2 - FIRST_ROWS, PAIR), lambda i: (i, 0, 0)),
         ],
         out_shape=[
             jax.ShapeDtypeStruct((heads, tokens, PAIR), qkv.dtype),
-            jax.ShapeDtypeStruct((heads, tokens // 2, PAIR), qkv.dtype),
+            jax.ShapeDtypeStruct((heads, FIRST_ROWS, PAIR), qkv.dtype),
+            jax.ShapeDtypeStruct((heads, tokens // 2 - FIRST_ROWS, PAIR), qkv.dtype),
         ],
         name="split_heads",
     )(qkv)
@@ -83,7 +87,9 @@
     return jnp.concatenate([stacked, jnp.zeros_like(stacked)], axis=1)
 
 
-def attend_kernel(list_ref, q_ref, prev_ref, own_ref, next_ref, o_ref, asked, raw, sems):
+def attend_kernel(
+    list_ref, first_ref, rest_ref, prev_ref, own_ref, next_ref, o_ref, asked, raw, sems
+):
     step = pl.program_id(0)
 
     @pl.when(step == 0)
@@ -93,7 +99,9 @@
             (src, raw.at[pl.ds(i * tiles, tiles)])
             for i, src in enumerate((prev_ref, own_ref, next_ref))
         ]
-        pairs.append((q_ref, asked))
+        rows = first_ref.shape[1]
+        pairs.append((first_ref, asked.at[:, pl.ds(0, rows)]))
+        pairs.append((rest_ref, asked.at[:, pl.ds(rows, rest_ref.shape[1])]))
         load_all(pairs, sems)
 
     count = list_ref.shape[1]
@@ -132,8 +140,8 @@
         held = following
 
 
-def attend(local_list, queries, before, own, after):
-    tiles, half, _ = queries.shape
+def attend(local_list, first, rest, before, own, after):
+    tiles, half = first.shape[0], first.shape[1] + rest.shape[1]
     tile_len = own.shape[1]
     hbm = pl.BlockSpec(memory_space=pl.ANY)
     return pl.pallas_call(
@@ -141,28 +149,34 @@
         grid_spec=pltpu.PrefetchScalarGridSpec(
             num_scalar_prefetch=1,
             grid=(tiles // STEP_TILES,),
-            in_specs=[hbm] * 4,
+            in_specs=[hbm] * 5,
             out_specs=pl.BlockSpec((STEP_TILES, half, PAIR), lambda i, _: (i, 0, 0)),
             scratch_shapes=[
                 pltpu.VMEM((tiles, half, PAIR), jnp.bfloat16),
                 pltpu.VMEM((3 * tiles, tile_len, PAIR), jnp.bfloat16),
-                pltpu.SemaphoreType.DMA((4,)),
+                pltpu.SemaphoreType.DMA((5,)),
             ],
         ),
-        out_shape=jax.ShapeDtypeStruct((tiles, half, PAIR), queries.dtype),
+        out_shape=jax.ShapeDtypeStruct((tiles, half, PAIR), rest.dtype),
         compiler_params=pltpu.CompilerParams(vmem_limit_bytes=32 * 2**20),
         name="attend",
-    )(local_list, queries, before, own, after)
+    )(local_list, first, rest, before, own, after)
 
 
 def exchange(array):
     return lax.all_to_all(array, "uly", split_axis=0, concat_axis=0, tiled=True)
 
 
-def exchange_in_two(array):
-    first = exchange(array[:, :FIRST_ROWS])
-    array, first = lax.optimization_barrier((array, first))
-    return jnp.concatenate([first, exchange(array[:, FIRST_ROWS:])], axis=1)
+def send_early(kv, first):
+    tokens = kv.shape[1]
+    both = exchange(jnp.concatenate([kv, first], axis=1))
+    return both[:, :tokens], both[:, tokens:]
+
+
+def send_late(kv, first):
+    first = exchange(first)
+    kv, first = lax.optimization_barrier((kv, first))
+    return exchange(kv), first
 
 
 def late_frame(frame):
@@ -172,18 +186,18 @@
 def on_device(qkv, tile_list):
     frames = lax.axis_size("blk")
     frame = lax.axis_index("blk")
-    kv, queries = split_heads(qkv)
-    kv = lax.cond(late_frame(frame) == 0, exchange, exchange_in_two, kv)
+    kv, first, rest = split_heads(qkv)
+    kv, first = lax.cond(late_frame(frame) == 0, send_early, send_late, kv, first)
     far = lax.ppermute(kv, "blk", [p for i in range(1, frames - 1, 2) for p in ((i, i + 1), (i + 1, i))])
-    queries = exchange(queries)
+    rest = exchange(rest)
     near = lax.ppermute(kv, "blk", [p for i in range(0, frames, 2) for p in ((i, i + 1), (i + 1, i))])
-    far, queries, tile_list = lax.optimization_barrier((far, queries, tile_list))
+    far, rest, tile_list = lax.optimization_barrier((far, rest, tile_list))
     frame_tiles = tile_list.shape[0]
     their_frame, place = tile_list // frame_tiles, tile_list % frame_tiles
     step = their_frame - frame
     slot = 1 - jnp.where(frame % 2 == 0, step, -step)
     local_list = slot * frame_tiles + place
-    result = attend(local_list, queries, near, kv, far)
+    result = attend(local_list, first, rest, near, kv, far)
     return merge_heads(exchange(result))
 
 

time: 148 us -> 151 us (1.020)
  blocking collectives: 88.4 us -> 92.6 us
  waiting for transfers between devices: 17.6 us -> 20.7 us
  starting transfers between devices: 10.9 us -> 7.86 us
  other arithmetic: 1.62 us -> 0.03 us
    all_to_all x3, blocking collectives: 88.4 us -> 92.6 us  [exchange(): return lax.all_to_all(array, 'uly', split_axis=0, concat_axis=0, tiled=True)]
    all_to_all x1, waiting for transfers between devices: 17.5 us -> 20.7 us  [exchange(): return lax.all_to_all(array, 'uly', split_axis=0, concat_axis=0, tiled=True)]
    all_to_all x1, starting transfers between devices: 6.37 us -> 4.75 us  [exchange(): return lax.all_to_all(array, 'uly', split_axis=0, concat_axis=0, tiled=True)]
    concatenate x1 -> x0, other arithmetic: 1.59 us -> none  [exchange_in_two(): return jnp.concatenate([first, exchange(array[:, FIRST_ROWS:])], axis=1)]
where the time goes in v9:
time: 151 us; the launch traced here: 150 us
  blocking collectives  92.6 us (61%)
  Pallas kernels  28.8 us (19%)
  waiting for transfers between devices  20.7 us (14%)
  starting transfers between devices  7.86 us (5%)
    all_to_all x3, blocking collectives, exchange(): return lax.all_to_all(array, 'uly', split_axis=0, concat_axis=0, tiled=True)  92.6 us
    pallas_call x1, Pallas kernels, attend(): pl.pallas_call(attend_kernel, grid_spec=pltpu.PrefetchScalarGridSpec(num_...  24.3 us
    all_to_all x1, waiting for transfers between devices, exchange(): return lax.all_to_all(array, 'uly', split_axis=0, concat_axis=0, tiled=True)  20.7 us
    all_to_all x1, starting transfers between devices, exchange(): return lax.all_to_all(array, 'uly', split_axis=0, concat_axis=0, tiled=True)  4.75 us
    pallas_call x1, Pallas kernels, split_heads(): pl.pallas_call(split_kernel, grid=(heads // group,), in_specs=[pl.BlockSp...  3.3 us
  transfers between devices with their start and end apart: 3, of which 1 were waited for; matrix products, arithmetic and copies ran while one was open for 0% of the time, Pallas kernels for 0%

profile of v9, /device:TPU:37, one launch (start us, length us, event | category | flops | bytes accessed | tf_op | source)
XLA Modules:
  0.0 150.1 jit_solution(7053108319925959032)
XLA Ops:
  0.0 3.3 %split_heads.1 = (bf16[32,256,128]{2,1,0:T(8,128)(2,1)S(1)}, bf16[32,8,128]{2,1,0:T(8,128)(2,1)S(1)}, bf16[32,120,128]{2,1,0:T(8,128)(2,1)}) custom-call(bf16[256,6144]{1,0:T(8,128)(2,1)} %qkv_ref.1), custom_call_target="tpu_custom_call" | custom-call | tf_op jit(solution)/shard_map/split_heads/pallas_call | solution.py:34
  3.3 0.0 copy-start
  3.3 64.4 %conditional.1 = (bf16[32,256,128]{2,1,0:T(8,128)(2,1)}, bf16[32,8,128]{2,1,0:T(8,128)(2,1)S(1)}) conditional(s32[]{:T(128)} %convert_element_type.3, (bf16[32,8,128]{2,1,0:T(8,128)(2,1)S(1)}, bf16[32,256,128]{2,1,0:T(8,128)(2,1)S(1)}) %tuple.15, (bf16[32,256,128]{2,1,0:T(8,128)(2,1)S(1)}, bf16[32,8,128]{2,1,0:T(8,128)(2,1)S(1)}) %tuple.16), branch_computations={%region_0.1_spmd, %region_1.2_spmd} | conditional | flops 4325376 | bytes 12976144 | solution.py:190
  3.3 18.9 %all_to_all.22 = bf16[32,8,128]{2,1,0:T(8,128)(2,1)S(1)} all-to-all(bf16[32,8,128]{2,1,0:T(8,128)(2,1)S(1)} %get-tuple-element.14), channel_id=1, replica_groups=mesh['uly'=32,'blk'=8] {'uly'}, dimensions={0} | all-to-all | bytes 131072 | tf_op jit(solution)/shard_map/cond/branch_0_fun/all_to_all | solution.py:167
  22.3 45.5 %all_to_all.23 = bf16[32,256,128]{2,1,0:T(8,128)(2,1)} all-to-all(bf16[32,256,128]{2,1,0:T(8,128)(2,1)S(1)} %get-tuple-element.15), channel_id=1, replica_groups=mesh['uly'=32,'blk'=8] {'uly'}, dimensions={0} | all-to-all | bytes 4194304 | tf_op jit(solution)/shard_map/cond/branch_0_fun/all_to_all | solution.py:167
  67.7 2.8 %collective-permute-start = (bf16[32,256,128]{2,1,0:T(8,128)(2,1)}, bf16[32,256,128]{2,1,0:T(8,128)(2,1)S(1)}, u32[]{:S(2)}, u32[]{:S(2)}) collective-permute-start(bf16[32,256,128]{2,1,0:T(8,128)(2,1)} %get-tuple-element.29.own_ref), channel_id=1, source_target_pairs={{1,2},{2,1},{3,4},{4,3},{5,6},{6,5},{9,10},{10,9},{11,12},{12,11},... | collective-permute-start | bytes 6291464 | tf_op jit(solution)/shard_map/ppermute | solution.py:191
  70.5 4.8 %all-to-all-start.3 = ((bf16[32,120,128]{2,1,0:T(8,128)(2,1)}), bf16[32,120,128]{2,1,0:T(8,128)(2,1)S(1)}, u32[]{:S(2)}, u32[]{:S(2)}) async-start(bf16[32,120,128]{2,1,0:T(8,128)(2,1)} %get-tuple-element.30), calls=%async_computation.3 | async-start | bytes 1966080 | tf_op jit(solution)/shard_map/all_to_all | solution.py:167
  75.3 0.3 collective-permute-start.1
  75.6 20.7 %all-to-all-done.3.rest_ref = bf16[32,120,128]{2,1,0:T(8,128)(2,1)S(1)} async-done(((bf16[32,120,128]{2,1,0:T(8,128)(2,1)}), bf16[32,120,128]{2,1,0:T(8,128)(2,1)S(1)}, u32[]{:S(2)}, u32[]{:S(2)}) %all-to-all-start.3) | async-done | bytes 983072 | tf_op jit(solution)/shard_map/all_to_all | solution.py:167
  96.3 0.0 collective-permute-done.next_ref
  96.3 0.0 copy-done
  96.3 0.1 copy.3
  96.4 0.0 collective-permute-done.1.prev_ref
  96.4 24.3 %attend.1 = bf16[32,128,128]{2,1,0:T(8,128)(2,1)S(1)} custom-call(s32[32,8]{1,0:T(8,128)S(1)} %fusion.3.list_ref, bf16[32,8,128]{2,1,0:T(8,128)(2,1)S(1)} %get-tuple-element.32.first_ref, bf16[32,120,128]{2,1,0:T(8,128)(2,1)S(1)} %all-to-all-done.3.rest_ref, bf16[32,256,128]{2,1,0:T(8,128)(2,1)} %collective-permute-done.1.prev_ref, ...), custom_call_target="tpu_custom_call" | custom-call | tf_op jit(solution)/shard_map/attend/pallas_call | solution.py:147
  120.7 28.2 %all_to_all.25.o_ref = bf16[32,128,128]{2,1,0:T(8,128)(2,1)S(1)} all-to-all(bf16[32,128,128]{2,1,0:T(8,128)(2,1)S(1)} %attend.1), channel_id=1, replica_groups=mesh['uly'=32,'blk'=8] {'uly'}, dimensions={0} | all-to-all | bytes 2097152 | tf_op jit(solution)/shard_map/all_to_all | solution.py:167
  148.9 1.3 merge_heads.1
  (1 shorter events, 0.0 us)
Async XLA Ops:
  3.3 93.0 %copy-start = (s32[32,8]{0,1:T(8,128)S(1)}, s32[32,8]{0,1:T(8,128)}, u32[]{:S(2)}) copy-start(s32[32,8]{0,1:T(8,128)} %param.5) | copy-start | bytes 3076
  67.7 28.6 %collective-permute-start = (bf16[32,256,128]{2,1,0:T(8,128)(2,1)}, bf16[32,256,128]{2,1,0:T(8,128)(2,1)S(1)}, u32[]{:S(2)}, u32[]{:S(2)}) collective-permute-start(bf16[32,256,128]{2,1,0:T(8,128)(2,1)} %get-tuple-element.29.own_ref), channel_id=1, source_target_pairs={{1,2},{2,1},{3,4},{4,3},{5,6},{6,5},{9,10},{10,9},{11,12},{12,11},... | collective-permute-start | bytes 6291464 | tf_op jit(solution)/shard_map/ppermute | solution.py:191
  70.5 25.7 %all-to-all-start.3 = ((bf16[32,120,128]{2,1,0:T(8,128)(2,1)}), bf16[32,120,128]{2,1,0:T(8,128)(2,1)S(1)}, u32[]{:S(2)}, u32[]{:S(2)}) async-start(bf16[32,120,128]{2,1,0:T(8,128)(2,1)} %get-tuple-element.30), calls=%async_computation.3 | async-start | bytes 1966080 | tf_op jit(solution)/shard_map/all_to_all | solution.py:167
  75.3 21.1 %collective-permute-start.1 = (bf16[32,256,128]{2,1,0:T(8,128)(2,1)}, bf16[32,256,128]{2,1,0:T(8,128)(2,1)}, u32[]{:S(2)}, u32[]{:S(2)}) collective-permute-start(bf16[32,256,128]{2,1,0:T(8,128)(2,1)} %get-tuple-element.29.own_ref), channel_id=1, source_target_pairs={{0,1},{1,0},{2,3},{3,2},{4,5},{5,4},{6,7},{7,6},{8,9},{9,8},{10,11... | collective-permute-start | bytes 6291464 | tf_op jit(solution)/shard_map/ppermute | solution.py:193

commit v10 on v8

--- a/solution.py
+++ b/solution.py
@@ -10,37 +10,56 @@
 SPLIT_HEADS = 16
 STEP_TILES = 16
 FIRST_ROWS = 8
-
-
-def split_kernel(qkv_ref, kv_ref, q_ref):
-    half = qkv_ref.shape[0] // 2
-    for pair in range(kv_ref.shape[0] // 2):
-        base = pair * 6 * HEAD_DIM
-        for odd in range(2):
-            col = base + odd * 3 * HEAD_DIM
-            head = 2 * pair + odd
-            kv_ref[head] = qkv_ref[:, col + HEAD_DIM : col + 3 * HEAD_DIM]
-            q_ref[head] = jnp.concatenate(
-                [qkv_ref[:half, col : col + HEAD_DIM], qkv_ref[half:, col : col + HEAD_DIM]], axis=1
+SPLIT_CHUNK = 8
+SPLIT_VMEM = 57 * 2**20
+
+
+def split_kernel(qkv_ref, kv_ref, q_ref, landed, packed, sems, q_sems):
+    chunks, tokens, width = landed.shape
+    half = tokens // 2
+    copies = [
+        pltpu.make_async_copy(qkv_ref.at[:, pl.ds(i * width, width)], landed.at[i], sems.at[i])
+        for i in range(chunks)
+    ]
+    for copy in copies:
+        copy.start()
+    heads = width // (3 * HEAD_DIM)
+    q_copies = []
+    for i in range(chunks):
+        copies[i].wait()
+        for j in range(heads):
+            col = j * 3 * HEAD_DIM
+            head = i * heads + j
+            kv_ref[head] = landed[i, :, col + HEAD_DIM : col + 3 * HEAD_DIM]
+            packed[head] = jnp.concatenate(
+                [landed[i, :half, col : col + HEAD_DIM], landed[i, half:, col : col + HEAD_DIM]], axis=1
             )
+        part = pl.ds(i * heads, heads)
+        q_copies.append(pltpu.make_async_copy(packed.at[part], q_ref.at[part], q_sems.at[i]))
+        q_copies[i].start()
+    for copy in q_copies:
+        copy.wait()
 
 
 def split_heads(qkv):
     tokens, width = qkv.shape
     heads = width // (3 * HEAD_DIM)
-    group = SPLIT_HEADS
+    chunks = heads // SPLIT_CHUNK
     return pl.pallas_call(
         split_kernel,
-        grid=(heads // group,),
-        in_specs=[pl.BlockSpec((tokens, group * 3 * HEAD_DIM), lambda i: (0, i))],
-        out_specs=[
-            pl.BlockSpec((group, tokens, PAIR), lambda i: (i, 0, 0)),
-            pl.BlockSpec((group, tokens // 2, PAIR), lambda i: (i, 0, 0)),
+        in_specs=[pl.BlockSpec(memory_space=pltpu.HBM)],
+        out_specs=[pl.BlockSpec(memory_space=pltpu.VMEM), pl.BlockSpec(memory_space=pltpu.HBM)],
+        out_shape=[
+            pltpu.VMEM((heads, tokens, PAIR), qkv.dtype),
+            pltpu.HBM((heads, tokens // 2, PAIR), qkv.dtype),
         ],
-        out_shape=[
-            jax.ShapeDtypeStruct((heads, tokens, PAIR), qkv.dtype),
-            jax.ShapeDtypeStruct((heads, tokens // 2, PAIR), qkv.dtype),
+        scratch_shapes=[
+            pltpu.VMEM((chunks, tokens, width // chunks), qkv.dtype),
+            pltpu.VMEM((heads, tokens // 2, PAIR), qkv.dtype),
+            pltpu.SemaphoreType.DMA((chunks,)),
+            pltpu.SemaphoreType.DMA((chunks,)),
         ],
+        compiler_params=pltpu.CompilerParams(vmem_limit_bytes=SPLIT_VMEM),
         name="split_heads",
     )(qkv)
 

time: 148 us -> 148 us (level)
  no operation moved by 1% of the time
where the time goes in v10:
time: 148 us
  blocking collectives  88.4 us (60%)
  Pallas kernels  28.7 us (19%)
  waiting for transfers between devices  17.6 us (12%)
  starting transfers between devices  11 us (7%)
  other arithmetic  1.62 us (1%)
    all_to_all x3, blocking collectives, exchange(): return lax.all_to_all(array, 'uly', split_axis=0, concat_axis=0, tiled=True)  88.4 us
    pallas_call x1, Pallas kernels, attend(): pl.pallas_call(attend_kernel, grid_spec=pltpu.PrefetchScalarGridSpec(num_...  24.3 us
    all_to_all x1, waiting for transfers between devices, exchange(): return lax.all_to_all(array, 'uly', split_axis=0, concat_axis=0, tiled=True)  17.5 us
    all_to_all x1, starting transfers between devices, exchange(): return lax.all_to_all(array, 'uly', split_axis=0, concat_axis=0, tiled=True)  6.52 us
    ppermute x1, starting transfers between devices, on_device(): lax.ppermute(kv, 'blk', [p for i in range(1, frames - 1, 2) for p in ((i,...  4.22 us
    pallas_call x1, Pallas kernels, split_heads(): pl.pallas_call(split_kernel, in_specs=[pl.BlockSpec(memory_space=pltpu.HB...  3.15 us
  transfers between devices with their start and end apart: 3, of which 1 were waited for; matrix products, arithmetic and copies ran while one was open for 0% of the time, Pallas kernels for 0%

profile of v10, /device:TPU:37, one launch (start us, length us, event | category | flops | bytes accessed | tf_op | source)
XLA Modules:
  0.0 147.6 jit_solution(13228975304462358082)
XLA Ops:
  0.0 3.1 %split_heads.1 = (bf16[32,256,128]{2,1,0:T(8,128)(2,1)S(1)}, bf16[32,128,128]{2,1,0:T(8,128)(2,1)}) custom-call(bf16[256,6144]{1,0:T(8,128)(2,1)} %qkv_ref.1), custom_call_target="tpu_custom_call" | custom-call | tf_op jit(solution)/shard_map/split_heads/pallas_call | solution.py:48
  3.2 64.4 %conditional.1 = (bf16[32,256,128]{2,1,0:T(8,128)(2,1)}) conditional(s32[]{:T(128)} %convert_element_type.3, bf16[32,256,128]{2,1,0:T(8,128)(2,1)S(1)} %get-tuple-element.17, bf16[32,256,128]{2,1,0:T(8,128)(2,1)S(1)} %get-tuple-element.17), branch_computations={%region_0.1_spmd, %region_1.2_spmd} | conditional | flops 4194304 | bytes 12582920 | solution.py:195
  3.2 19.2 %all_to_all.22 = bf16[32,8,128]{2,1,0:T(8,128)(2,1)S(1)} all-to-all(bf16[32,8,128]{2,1,0:T(8,128)(2,1)S(1)} %slice.4), channel_id=1, replica_groups=mesh['uly'=32,'blk'=8] {'uly'}, dimensions={0} | all-to-all | bytes 131072 | tf_op jit(solution)/shard_map/cond/branch_0_fun/all_to_all | solution.py:178
  22.4 0.1 slice.5
  22.6 43.4 %all_to_all.23 = bf16[32,248,128]{2,1,0:T(8,128)(2,1)S(1)} all-to-all(bf16[32,248,128]{2,1,0:T(8,128)(2,1)S(1)} %slice.5), channel_id=1, replica_groups=mesh['uly'=32,'blk'=8] {'uly'}, dimensions={0} | all-to-all | bytes 4063232 | tf_op jit(solution)/shard_map/cond/branch_0_fun/all_to_all | solution.py:178
  66.0 1.6 %pad_maximum_fusion = bf16[32,256,128]{2,1,0:T(8,128)(2,1)} fusion(bf16[32,248,128]{2,1,0:T(8,128)(2,1)S(1)} %all_to_all.23, bf16[32,8,128]{2,1,0:T(8,128)(2,1)S(1)} %all_to_all.22), kind=kLoop, calls=%fused_computation | loop fusion | flops 4194304 | bytes 4194304 | tf_op jit(solution)/shard_map/cond/branch_0_fun/concatenate | solution.py:184
  67.6 0.0 copy-start
  67.6 4.2 %collective-permute-start = (bf16[32,256,128]{2,1,0:T(8,128)(2,1)}, bf16[32,256,128]{2,1,0:T(8,128)(2,1)S(1)}, u32[]{:S(2)}, u32[]{:S(2)}) collective-permute-start(bf16[32,256,128]{2,1,0:T(8,128)(2,1)} %get-tuple-element.22.own_ref), channel_id=1, source_target_pairs={{1,2},{2,1},{3,4},{4,3},{5,6},{6,5},{9,10},{10,9},{11,12},{12,11},... | collective-permute-start | bytes 6291464 | tf_op jit(solution)/shard_map/ppermute | solution.py:196
  71.8 6.5 %all-to-all-start.3 = ((bf16[32,128,128]{2,1,0:T(8,128)(2,1)}), bf16[32,128,128]{2,1,0:T(8,128)(2,1)S(1)}, u32[]{:S(2)}, u32[]{:S(2)}) async-start(bf16[32,128,128]{2,1,0:T(8,128)(2,1)} %get-tuple-element.18), calls=%async_computation.3 | async-start | bytes 2097152 | tf_op jit(solution)/shard_map/all_to_all | solution.py:178
  78.3 0.3 collective-permute-start.1
  78.6 17.5 %all-to-all-done.3.q_ref = bf16[32,128,128]{2,1,0:T(8,128)(2,1)S(1)} async-done(((bf16[32,128,128]{2,1,0:T(8,128)(2,1)}), bf16[32,128,128]{2,1,0:T(8,128)(2,1)S(1)}, u32[]{:S(2)}, u32[]{:S(2)}) %all-to-all-start.3) | async-done | bytes 1048608 | tf_op jit(solution)/shard_map/all_to_all | solution.py:178
  96.2 0.0 collective-permute-done.next_ref
  96.2 0.0 copy-done
  96.2 0.1 copy.3
  96.3 0.0 collective-permute-done.1.prev_ref
  96.3 24.3 %attend.1 = bf16[32,128,128]{2,1,0:T(8,128)(2,1)S(1)} custom-call(s32[32,8]{1,0:T(8,128)S(1)} %fusion.3.list_ref, bf16[32,128,128]{2,1,0:T(8,128)(2,1)S(1)} %all-to-all-done.3.q_ref, bf16[32,256,128]{2,1,0:T(8,128)(2,1)} %collective-permute-done.1.prev_ref, bf16[32,256,128]{2,1,0:T(8,128)(2,1)} %get-tuple-element.22.own_ref, ...), custom_call_target="tpu_custom_call" | custom-call | tf_op jit(solution)/shard_map/attend/pallas_call | solution.py:158
  120.5 25.8 %all_to_all.25.o_ref = bf16[32,128,128]{2,1,0:T(8,128)(2,1)S(1)} all-to-all(bf16[32,128,128]{2,1,0:T(8,128)(2,1)S(1)} %attend.1), channel_id=1, replica_groups=mesh['uly'=32,'blk'=8] {'uly'}, dimensions={0} | all-to-all | bytes 2097152 | tf_op jit(solution)/shard_map/all_to_all | solution.py:178
  146.3 1.3 merge_heads.1
  (2 shorter events, 0.0 us)
Async XLA Ops:
  67.6 28.6 %copy-start = (s32[32,8]{0,1:T(8,128)S(1)}, s32[32,8]{0,1:T(8,128)}, u32[]{:S(2)}) copy-start(s32[32,8]{0,1:T(8,128)} %param.5) | copy-start | bytes 3076
  67.6 28.6 %collective-permute-start = (bf16[32,256,128]{2,1,0:T(8,128)(2,1)}, bf16[32,256,128]{2,1,0:T(8,128)(2,1)S(1)}, u32[]{:S(2)}, u32[]{:S(2)}) collective-permute-start(bf16[32,256,128]{2,1,0:T(8,128)(2,1)} %get-tuple-element.22.own_ref), channel_id=1, source_target_pairs={{1,2},{2,1},{3,4},{4,3},{5,6},{6,5},{9,10},{10,9},{11,12},{12,11},... | collective-permute-start | bytes 6291464 | tf_op jit(solution)/shard_map/ppermute | solution.py:196
  71.8 24.4 %all-to-all-start.3 = ((bf16[32,128,128]{2,1,0:T(8,128)(2,1)}), bf16[32,128,128]{2,1,0:T(8,128)(2,1)S(1)}, u32[]{:S(2)}, u32[]{:S(2)}) async-start(bf16[32,128,128]{2,1,0:T(8,128)(2,1)} %get-tuple-element.18), calls=%async_computation.3 | async-start | bytes 2097152 | tf_op jit(solution)/shard_map/all_to_all | solution.py:178
  78.3 18.0 %collective-permute-start.1 = (bf16[32,256,128]{2,1,0:T(8,128)(2,1)}, bf16[32,256,128]{2,1,0:T(8,128)(2,1)}, u32[]{:S(2)}, u32[]{:S(2)}) collective-permute-start(bf16[32,256,128]{2,1,0:T(8,128)(2,1)} %get-tuple-element.22.own_ref), channel_id=1, source_target_pairs={{0,1},{1,0},{2,3},{3,2},{4,5},{5,4},{6,7},{7,6},{8,9},{9,8},{10,11... | collective-permute-start | bytes 6291464 | tf_op jit(solution)/shard_map/ppermute | solution.py:198

commit v11 on v8

--- a/solution.py
+++ b/solution.py
@@ -159,10 +159,33 @@
     return lax.all_to_all(array, "uly", split_axis=0, concat_axis=0, tiled=True)
 
 
+def join_kernel(first_ref, rest_ref, out_ref, sems):
+    rows = first_ref.shape[1]
+    pairs = [
+        (first_ref, out_ref.at[:, pl.ds(0, rows)]),
+        (rest_ref, out_ref.at[:, pl.ds(rows, rest_ref.shape[1])]),
+    ]
+    load_all(pairs, sems)
+
+
+def join_rows(first, rest):
+    hbm = pl.BlockSpec(memory_space=pl.ANY)
+    rows = first.shape[1] + rest.shape[1]
+    return pl.pallas_call(
+        join_kernel,
+        in_specs=[hbm, hbm],
+        out_specs=hbm,
+        out_shape=jax.ShapeDtypeStruct((first.shape[0], rows, first.shape[2]), first.dtype),
+        scratch_shapes=[pltpu.SemaphoreType.DMA((2,))],
+        compiler_params=pltpu.CompilerParams(vmem_limit_bytes=2**20),
+        name="join_rows",
+    )(first, rest)
+
+
 def exchange_in_two(array):
     first = exchange(array[:, :FIRST_ROWS])
     array, first = lax.optimization_barrier((array, first))
-    return jnp.concatenate([first, exchange(array[:, FIRST_ROWS:])], axis=1)
+    return join_rows(first, exchange(array[:, FIRST_ROWS:]))
 
 
 def late_frame(frame):

time: 148 us -> 148 us (level)
  other arithmetic: 1.62 us -> 0.03 us
    concatenate x1 -> x0, other arithmetic: 1.59 us -> none  [exchange_in_two(): return jnp.concatenate([first, exchange(array[:, FIRST_ROWS:])], axis=1)]
where the time goes in v11:
time: 148 us; the launch traced here: 147 us
  blocking collectives  88.2 us (60%)
  Pallas kernels  30.1 us (20%)
  waiting for transfers between devices  17.7 us (12%)
  starting transfers between devices  10.8 us (7%)
    all_to_all x3, blocking collectives, exchange(): return lax.all_to_all(array, 'uly', split_axis=0, concat_axis=0, tiled=True)  88.2 us
    pallas_call x1, Pallas kernels, attend(): pl.pallas_call(attend_kernel, grid_spec=pltpu.PrefetchScalarGridSpec(num_...  24.3 us
    all_to_all x1, waiting for transfers between devices, exchange(): return lax.all_to_all(array, 'uly', split_axis=0, concat_axis=0, tiled=True)  17.7 us
    all_to_all x1, starting transfers between devices, exchange(): return lax.all_to_all(array, 'uly', split_axis=0, concat_axis=0, tiled=True)  6.43 us
    ppermute x1, starting transfers between devices, on_device(): lax.ppermute(kv, 'blk', [p for i in range(1, frames - 1, 2) for p in ((i,...  4.12 us
    pallas_call x1, Pallas kernels, split_heads(): pl.pallas_call(split_kernel, grid=(heads // group,), in_specs=[pl.BlockSp...  3.31 us
  transfers between devices with their start and end apart: 3, of which 1 were waited for; matrix products, arithmetic and copies ran while one was open for 0% of the time, Pallas kernels for 0%

profile of v11, /device:TPU:37, one launch (start us, length us, event | category | flops | bytes accessed | tf_op | source)
XLA Modules:
  0.0 147.3 jit_solution(17646549687506788036)
XLA Ops:
  0.0 3.3 %split_heads.1 = (bf16[32,256,128]{2,1,0:T(8,128)(2,1)S(1)}, bf16[32,128,128]{2,1,0:T(8,128)(2,1)}) custom-call(bf16[256,6144]{1,0:T(8,128)(2,1)} %qkv_ref.1), custom_call_target="tpu_custom_call" | custom-call | tf_op jit(solution)/shard_map/split_heads/pallas_call | solution.py:32
  3.3 64.1 %conditional.1 = (bf16[32,256,128]{2,1,0:T(8,128)(2,1)}) conditional(s32[]{:T(128)} %convert_element_type.3, bf16[32,256,128]{2,1,0:T(8,128)(2,1)S(1)} %get-tuple-element.17, bf16[32,256,128]{2,1,0:T(8,128)(2,1)S(1)} %get-tuple-element.17), branch_computations={%region_0.1_spmd, %region_1.2_spmd} | conditional | bytes 8388616 | solution.py:199
  3.3 19.2 %all_to_all.22.first_ref = bf16[32,8,128]{2,1,0:T(8,128)(2,1)S(1)} all-to-all(bf16[32,8,128]{2,1,0:T(8,128)(2,1)S(1)} %slice.4), channel_id=1, replica_groups=mesh['uly'=32,'blk'=8] {'uly'}, dimensions={0} | all-to-all | bytes 131072 | tf_op jit(solution)/shard_map/cond/branch_0_fun/all_to_all | solution.py:159
  22.6 0.1 slice.5
  22.7 43.4 %all_to_all.23.rest_ref = bf16[32,248,128]{2,1,0:T(8,128)(2,1)S(1)} all-to-all(bf16[32,248,128]{2,1,0:T(8,128)(2,1)S(1)} %slice.5), channel_id=1, replica_groups=mesh['uly'=32,'blk'=8] {'uly'}, dimensions={0} | all-to-all | bytes 4063232 | tf_op jit(solution)/shard_map/cond/branch_0_fun/all_to_all | solution.py:159
  66.1 1.3 join_rows.1
  67.4 0.0 copy-start
  67.4 4.1 %collective-permute-start = (bf16[32,256,128]{2,1,0:T(8,128)(2,1)}, bf16[32,256,128]{2,1,0:T(8,128)(2,1)S(1)}, u32[]{:S(2)}, u32[]{:S(2)}) collective-permute-start(bf16[32,256,128]{2,1,0:T(8,128)(2,1)} %get-tuple-element.22.own_ref), channel_id=1, source_target_pairs={{1,2},{2,1},{3,4},{4,3},{5,6},{6,5},{9,10},{10,9},{11,12},{12,11},... | collective-permute-start | bytes 6291464 | tf_op jit(solution)/shard_map/ppermute | solution.py:200
  71.6 6.4 %all-to-all-start.3 = ((bf16[32,128,128]{2,1,0:T(8,128)(2,1)}), bf16[32,128,128]{2,1,0:T(8,128)(2,1)S(1)}, u32[]{:S(2)}, u32[]{:S(2)}) async-start(bf16[32,128,128]{2,1,0:T(8,128)(2,1)} %get-tuple-element.18), calls=%async_computation.3 | async-start | bytes 2097152 | tf_op jit(solution)/shard_map/all_to_all | solution.py:159
  78.0 0.3 collective-permute-start.1
  78.3 17.7 %all-to-all-done.3.q_ref = bf16[32,128,128]{2,1,0:T(8,128)(2,1)S(1)} async-done(((bf16[32,128,128]{2,1,0:T(8,128)(2,1)}), bf16[32,128,128]{2,1,0:T(8,128)(2,1)S(1)}, u32[]{:S(2)}, u32[]{:S(2)}) %all-to-all-start.3) | async-done | bytes 1048608 | tf_op jit(solution)/shard_map/all_to_all | solution.py:159
  96.0 0.0 collective-permute-done.next_ref
  96.0 0.0 copy-done
  96.0 0.1 copy.3
  96.1 0.0 collective-permute-done.1.prev_ref
  96.1 24.3 %attend.1 = bf16[32,128,128]{2,1,0:T(8,128)(2,1)S(1)} custom-call(s32[32,8]{1,0:T(8,128)S(1)} %fusion.3.list_ref, bf16[32,128,128]{2,1,0:T(8,128)(2,1)S(1)} %all-to-all-done.3.q_ref, bf16[32,256,128]{2,1,0:T(8,128)(2,1)} %collective-permute-done.1.prev_ref, bf16[32,256,128]{2,1,0:T(8,128)(2,1)} %get-tuple-element.22.own_ref, ...), custom_call_target="tpu_custom_call" | custom-call | tf_op jit(solution)/shard_map/attend/pallas_call | solution.py:139
  120.4 25.6 %all_to_all.25.o_ref = bf16[32,128,128]{2,1,0:T(8,128)(2,1)S(1)} all-to-all(bf16[32,128,128]{2,1,0:T(8,128)(2,1)S(1)} %attend.1), channel_id=1, replica_groups=mesh['uly'=32,'blk'=8] {'uly'}, dimensions={0} | all-to-all | bytes 2097152 | tf_op jit(solution)/shard_map/all_to_all | solution.py:159
  146.0 1.3 merge_heads.1
  (2 shorter events, 0.0 us)
Async XLA Ops:
  67.4 28.6 %copy-start = (s32[32,8]{0,1:T(8,128)S(1)}, s32[32,8]{0,1:T(8,128)}, u32[]{:S(2)}) copy-start(s32[32,8]{0,1:T(8,128)} %param.5) | copy-start | bytes 3076
  67.4 28.6 %collective-permute-start = (bf16[32,256,128]{2,1,0:T(8,128)(2,1)}, bf16[32,256,128]{2,1,0:T(8,128)(2,1)S(1)}, u32[]{:S(2)}, u32[]{:S(2)}) collective-permute-start(bf16[32,256,128]{2,1,0:T(8,128)(2,1)} %get-tuple-element.22.own_ref), channel_id=1, source_target_pairs={{1,2},{2,1},{3,4},{4,3},{5,6},{6,5},{9,10},{10,9},{11,12},{12,11},... | collective-permute-start | bytes 6291464 | tf_op jit(solution)/shard_map/ppermute | solution.py:200
  71.6 24.4 %all-to-all-start.3 = ((bf16[32,128,128]{2,1,0:T(8,128)(2,1)}), bf16[32,128,128]{2,1,0:T(8,128)(2,1)S(1)}, u32[]{:S(2)}, u32[]{:S(2)}) async-start(bf16[32,128,128]{2,1,0:T(8,128)(2,1)} %get-tuple-element.18), calls=%async_computation.3 | async-start | bytes 2097152 | tf_op jit(solution)/shard_map/all_to_all | solution.py:159
  78.0 18.1 %collective-permute-start.1 = (bf16[32,256,128]{2,1,0:T(8,128)(2,1)}, bf16[32,256,128]{2,1,0:T(8,128)(2,1)}, u32[]{:S(2)}, u32[]{:S(2)}) collective-permute-start(bf16[32,256,128]{2,1,0:T(8,128)(2,1)} %get-tuple-element.22.own_ref), channel_id=1, source_target_pairs={{0,1},{1,0},{2,3},{3,2},{4,5},{5,4},{6,7},{7,6},{8,9},{9,8},{10,11... | collective-permute-start | bytes 6291464 | tf_op jit(solution)/shard_map/ppermute | solution.py:202

commit v12 on v11

--- a/solution.py
+++ b/solution.py
@@ -189,7 +189,7 @@
 
 
 def late_frame(frame):
-    return (frame + 1) // 2 % 2
+    return (frame + 3) // 2 % 2
 
 
 def on_device(qkv, tile_list):

time: 148 us -> 147 us (level)
  the two profiles are of different devices: /device:TPU:37 before, /device:TPU:7 now
where the time goes in v12:
time: 147 us
  blocking collectives  90 us (61%)
  Pallas kernels  30.1 us (20%)
  waiting for transfers between devices  20 us (14%)
  starting transfers between devices  6.47 us (4%)
    all_to_all x3, blocking collectives, exchange(): return lax.all_to_all(array, 'uly', split_axis=0, concat_axis=0, tiled=True)  90 us
    pallas_call x1, Pallas kernels, attend(): pl.pallas_call(attend_kernel, grid_spec=pltpu.PrefetchScalarGridSpec(num_...  24.3 us
    all_to_all x1, waiting for transfers between devices, exchange(): return lax.all_to_all(array, 'uly', split_axis=0, concat_axis=0, tiled=True)  20 us
    all_to_all x1, starting transfers between devices, exchange(): return lax.all_to_all(array, 'uly', split_axis=0, concat_axis=0, tiled=True)  5.4 us
    pallas_call x1, Pallas kernels, split_heads(): pl.pallas_call(split_kernel, grid=(heads // group,), in_specs=[pl.BlockSp...  3.31 us
  transfers between devices with their start and end apart: 3, of which 1 were waited for; matrix products, arithmetic and copies ran while one was open for 0% of the time, Pallas kernels for 0%

profile of v12, /device:TPU:7, one launch (start us, length us, event | category | flops | bytes accessed | tf_op | source)
XLA Modules:
  0.0 147.0 jit_solution(6711390403278868057)
XLA Ops:
  0.0 3.3 %split_heads.1 = (bf16[32,256,128]{2,1,0:T(8,128)(2,1)S(1)}, bf16[32,128,128]{2,1,0:T(8,128)(2,1)}) custom-call(bf16[256,6144]{1,0:T(8,128)(2,1)} %qkv_ref.1), custom_call_target="tpu_custom_call" | custom-call | tf_op jit(solution)/shard_map/split_heads/pallas_call | solution.py:32
  3.3 63.8 %conditional.1 = (bf16[32,256,128]{2,1,0:T(8,128)(2,1)}) conditional(s32[]{:T(128)} %convert_element_type.3, bf16[32,256,128]{2,1,0:T(8,128)(2,1)S(1)} %get-tuple-element.17, bf16[32,256,128]{2,1,0:T(8,128)(2,1)S(1)} %get-tuple-element.17), branch_computations={%region_0.1_spmd, %region_1.2_spmd} | conditional | bytes 8388616 | solution.py:199
  3.3 19.9 %all_to_all.22.first_ref = bf16[32,8,128]{2,1,0:T(8,128)(2,1)S(1)} all-to-all(bf16[32,8,128]{2,1,0:T(8,128)(2,1)S(1)} %slice.4), channel_id=1, replica_groups=mesh['uly'=32,'blk'=8] {'uly'}, dimensions={0} | all-to-all | bytes 131072 | tf_op jit(solution)/shard_map/cond/branch_0_fun/all_to_all | solution.py:159
  23.2 0.1 slice.5
  23.4 42.4 %all_to_all.23.rest_ref = bf16[32,248,128]{2,1,0:T(8,128)(2,1)S(1)} all-to-all(bf16[32,248,128]{2,1,0:T(8,128)(2,1)S(1)} %slice.5), channel_id=1, replica_groups=mesh['uly'=32,'blk'=8] {'uly'}, dimensions={0} | all-to-all | bytes 4063232 | tf_op jit(solution)/shard_map/cond/branch_0_fun/all_to_all | solution.py:159
  65.8 1.3 join_rows.1
  67.1 0.0 copy-start
  67.1 0.8 collective-permute-start
  68.0 5.4 %all-to-all-start.3 = ((bf16[32,128,128]{2,1,0:T(8,128)(2,1)}), bf16[32,128,128]{2,1,0:T(8,128)(2,1)S(1)}, u32[]{:S(2)}, u32[]{:S(2)}) async-start(bf16[32,128,128]{2,1,0:T(8,128)(2,1)} %get-tuple-element.18), calls=%async_computation.3 | async-start | bytes 2097152 | tf_op jit(solution)/shard_map/all_to_all | solution.py:159
  73.4 0.3 collective-permute-start.1
  73.7 20.0 %all-to-all-done.3.q_ref = bf16[32,128,128]{2,1,0:T(8,128)(2,1)S(1)} async-done(((bf16[32,128,128]{2,1,0:T(8,128)(2,1)}), bf16[32,128,128]{2,1,0:T(8,128)(2,1)S(1)}, u32[]{:S(2)}, u32[]{:S(2)}) %all-to-all-start.3) | async-done | bytes 1048608 | tf_op jit(solution)/shard_map/all_to_all | solution.py:159
  93.6 0.0 collective-permute-done.next_ref
  93.7 0.0 copy-done
  93.7 0.1 copy.3
  93.8 0.0 collective-permute-done.1.prev_ref
  93.8 24.3 %attend.1 = bf16[32,128,128]{2,1,0:T(8,128)(2,1)S(1)} custom-call(s32[32,8]{1,0:T(8,128)S(1)} %fusion.3.list_ref, bf16[32,128,128]{2,1,0:T(8,128)(2,1)S(1)} %all-to-all-done.3.q_ref, bf16[32,256,128]{2,1,0:T(8,128)(2,1)} %collective-permute-done.1.prev_ref, bf16[32,256,128]{2,1,0:T(8,128)(2,1)} %get-tuple-element.22.own_ref, ...), custom_call_target="tpu_custom_call" | custom-call | tf_op jit(solution)/shard_map/attend/pallas_call | solution.py:139
  118.0 27.7 %all_to_all.25.o_ref = bf16[32,128,128]{2,1,0:T(8,128)(2,1)S(1)} all-to-all(bf16[32,128,128]{2,1,0:T(8,128)(2,1)S(1)} %attend.1), channel_id=1, replica_groups=mesh['uly'=32,'blk'=8] {'uly'}, dimensions={0} | all-to-all | bytes 2097152 | tf_op jit(solution)/shard_map/all_to_all | solution.py:159
  145.7 1.3 merge_heads.1
  (2 shorter events, 0.0 us)
Async XLA Ops:
  67.1 26.5 %copy-start = (s32[32,8]{0,1:T(8,128)S(1)}, s32[32,8]{0,1:T(8,128)}, u32[]{:S(2)}) copy-start(s32[32,8]{0,1:T(8,128)} %param.5) | copy-start | bytes 3076
  67.1 26.5 %collective-permute-start = (bf16[32,256,128]{2,1,0:T(8,128)(2,1)}, bf16[32,256,128]{2,1,0:T(8,128)(2,1)S(1)}, u32[]{:S(2)}, u32[]{:S(2)}) collective-permute-start(bf16[32,256,128]{2,1,0:T(8,128)(2,1)} %get-tuple-element.22.own_ref), channel_id=1, source_target_pairs={{1,2},{2,1},{3,4},{4,3},{5,6},{6,5},{9,10},{10,9},{11,12},{12,11},... | collective-permute-start | bytes 6291464 | tf_op jit(solution)/shard_map/ppermute | solution.py:200
  68.0 25.7 %all-to-all-start.3 = ((bf16[32,128,128]{2,1,0:T(8,128)(2,1)}), bf16[32,128,128]{2,1,0:T(8,128)(2,1)S(1)}, u32[]{:S(2)}, u32[]{:S(2)}) async-start(bf16[32,128,128]{2,1,0:T(8,128)(2,1)} %get-tuple-element.18), calls=%async_computation.3 | async-start | bytes 2097152 | tf_op jit(solution)/shard_map/all_to_all | solution.py:159
  73.4 20.4 %collective-permute-start.1 = (bf16[32,256,128]{2,1,0:T(8,128)(2,1)}, bf16[32,256,128]{2,1,0:T(8,128)(2,1)}, u32[]{:S(2)}, u32[]{:S(2)}) collective-permute-start(bf16[32,256,128]{2,1,0:T(8,128)(2,1)} %get-tuple-element.22.own_ref), channel_id=1, source_target_pairs={{0,1},{1,0},{2,3},{3,2},{4,5},{5,4},{6,7},{7,6},{8,9},{9,8},{10,11... | collective-permute-start | bytes 6291464 | tf_op jit(solution)/shard_map/ppermute | solution.py:202
